TPU v7x, 128 devices: a whole 4x4x4 slice. The times are simulated.
128 devices in a mesh: dp: 4 (over z), row: 8 (over x, core), col: 4 (over y).
Axes of the slice: x: 4, y: 4, z: 4, core: 2. Of those that a mesh axis runs over, the one named last changes fastest.
Arguments:
- hidden: bfloat16 [16384, 1280], P(('dp', 'row'), 'col'), may hold values from -0.15625 to 0.15625
- teacher: bfloat16 [16384, 1280], P(('dp', 'row'), 'col'), may hold values from -0.15625 to 0.15625
- valid_mask: int32 [16384], P(('dp', 'row')), may hold values from 0 to 1
- segments: int32 [4, 4096], P('dp'), may hold values from 0 to 2, never falling along the last dimension, each value on 1 to 2048 neighbouring positions
- query_weight: bfloat16 [1280, 1280], P(('dp', 'row'), 'col'), may hold values from -0.15625 to 0.15625
- key_weight: bfloat16 [1280, 1280], P(('dp', 'row'), 'col'), may hold values from -0.15625 to 0.15625
- value_weight: bfloat16 [1280, 1280], P(('dp', 'row'), 'col'), may hold values from -0.15625 to 0.15625
- out_weight: bfloat16 [1280, 1280], P('col', ('dp', 'row')), may hold values from -1.5 to 1.5
- gate_weight: bfloat16 [1280, 5120], P(('dp', 'row'), 'col'), may hold values from -0.15625 to 0.15625
- up_weight: bfloat16 [1280, 5120], P(('dp', 'row'), 'col'), may hold values from -0.15625 to 0.15625
- down_weight: bfloat16 [5120, 1280], P('col', ('dp', 'row')), may hold values from -0.078125 to 0.078125
- attention_rate: float32 [1280], P('col'), may hold values from 0.1 to 0.6
- feedforward_rate: float32 [1280], P('col'), may hold values from 0.1 to 0.6
- score_gain: float32 [1280], P('col'), may hold values from 1 to 1.8
- up_gain: float32 [5120], P('col'), may hold values from 0.5 to 2
- gate_gain: float32 [5120], P('col'), may hold values from 0.5 to 2
Outputs:
- loss: float32 [], replicated
- output: bfloat16 [16384, 1280], P(('dp', 'row'), 'col')
- hidden_grad: float32 [16384, 1280], P(('dp', 'row'), 'col')
- query_weight_grad: float32 [1280, 1280], P(('dp', 'row'), 'col')
- key_weight_grad: float32 [1280, 1280], P(('dp', 'row'), 'col')
- value_weight_grad: float32 [1280, 1280], P(('dp', 'row'), 'col')
- out_weight_grad: float32 [1280, 1280], P('col', ('dp', 'row'))
- gate_weight_grad: float32 [1280, 5120], P(('dp', 'row'), 'col')
- up_weight_grad: float32 [1280, 5120], P(('dp', 'row'), 'col')
- down_weight_grad: float32 [5120, 1280], P('col', ('dp', 'row'))
- attention_rate_grad: float32 [1280], P('col')
- feedforward_rate_grad: float32 [1280], P('col')
- score_gain_grad: float32 [1280], P('col')
- up_gain_grad: float32 [5120], P('col')
- gate_gain_grad: float32 [5120], P('col')
Inputs may be any that keep to these rules, and one draw needn't show every extreme that they name: `segments`: in each group, document numbers never fall along the tokens; each document has 1 to 2048 tokens, and one has exactly 2048.
All inputs are finite; a program needn't handle non-finite values.
Results may differ from a plain program's by a relative error of at most 0.025.
Values may be sent and summed in bfloat16 or wider, within the bound.
A program may use at most 128 MiB of HBM per device.

v0:
```python
import math

import jax
import jax.numpy as jnp
import numpy as np
from jax import lax
from jax.experimental import pallas as pl
from jax.experimental.pallas import tpu as pltpu
from jax.sharding import PartitionSpec as P

D = 1280
HEAD_DIM = 64
EPS = 1e-06
HEADS = 5
ROWS = 512
TOK = 128
COLS = 320
TILE = 256
F32 = jnp.float32
BF16 = jnp.bfloat16
MESH = pl.DeviceIdType.MESH
DMA = pltpu.SemaphoreType.DMA
VMEM = pltpu.VMEM
IN_VMEM = pl.BlockSpec(memory_space=pltpu.VMEM)
IN_SMEM = pl.BlockSpec(memory_space=pltpu.SMEM)
IN_PLACE = pl.BlockSpec(memory_space=pl.ANY)
LIMIT = 60 << 20


def params(collective=None):
    if collective is None:
        return pltpu.CompilerParams(vmem_limit_bytes=LIMIT)
    return pltpu.CompilerParams(
        collective_id=collective, has_side_effects=True, vmem_limit_bytes=LIMIT
    )


def spot():
    row = lax.axis_index("row")
    return lax.axis_index("dp"), lax.div(row, 2), lax.rem(row, 2), lax.axis_index("col")


def wrap(i):
    return lax.rem(i + 8, 4)


def device(z, x, c, y):
    return (z, 2 * x + c, y)


def meet(others):
    barrier = pltpu.get_barrier_semaphore()
    for other in others:
        pl.semaphore_signal(barrier, inc=1, device_id=other, device_id_type=MESH)
    pl.semaphore_wait(barrier, len(others))


def remote(src, dst, send_sem, recv_sem, to):
    return pltpu.make_async_remote_copy(
        src_ref=src,
        dst_ref=dst,
        send_sem=send_sem,
        recv_sem=recv_sem,
        device_id=to,
        device_id_type=MESH,
    )


def dot_nn(a, b):
    return lax.dot_general(a, b, (((1,), (0,)), ((), ())), preferred_element_type=F32)


def dot_nt(a, b):
    return lax.dot_general(a, b, (((1,), (1,)), ((), ())), preferred_element_type=F32)


def dot_tn(a, b):
    return lax.dot_general(a, b, (((0,), (0,)), ((), ())), preferred_element_type=F32)


class Tally:
    def __init__(self, src, accs, parts, send, recv):
        z, x, c, y = spot()
        self.src, self.accs, self.parts, self.send, self.recv = src, accs, parts, send, recv
        self.peers = [
            [device(z, wrap(x + d), c, y) for d in (1, 2, 3)],
            [device(wrap(z + d), x, c, y) for d in (1, 2, 3)],
            [device(z, x, 1 - c, y)],
        ]
        self.copies = []

    def start(self, stage):
        src = self.src if stage == 0 else self.accs.at[stage - 1]
        for d, peer in enumerate(self.peers[stage]):
            at = 3 * stage + d
            copy = remote(src, self.parts.at[at], self.send.at[at], self.recv.at[at], peer)
            copy.start()
            self.copies.append(copy)

    def finish(self, stage):
        src = self.src if stage == 0 else self.accs.at[stage - 1]
        total = src[...]
        for d in range(len(self.peers[stage])):
            self.copies[3 * stage + d].wait_recv()
            total = total + self.parts[3 * stage + d]
        self.accs[stage] = total

    def close(self):
        for copy in self.copies:
            copy.wait_send()


TALLY_PEERS = 7


def tally_scratch(shape):
    return [
        VMEM((3,) + shape, F32),
        VMEM((7,) + shape, F32),
        DMA((7,)),
        DMA((7,)),
    ]


def torus(z, x, c, y):
    def first(d):
        return device(wrap(z + c * d), wrap(x + (1 - c) * d), c, y)

    def second(d):
        return device(wrap(z + (1 - c) * d), wrap(x + c * d), c, y)

    at_first = x * (1 - c) + z * c
    at_second = z * (1 - c) + x * c

    def block(d1, d2):
        a1, a2 = wrap(at_first + d1), wrap(at_second + d2)
        return (1 - c) * (a2 * 4 + a1) + c * (a1 * 4 + a2)

    return first, second, block


def half_mask(half):
    lane = lax.broadcasted_iota(jnp.int32, (1, 128), 1)
    return (lane < 64) if half == 0 else (lane >= 64)


def key_place(h):
    return h // 2, h % 2


def value_place(h):
    return (HEADS + h) // 2, (HEADS + h) % 2


def pad_head(wide, at, half):
    group = wide[:, 128 * at : 128 * at + 128]
    return jnp.where(half_mask(half), group, jnp.zeros_like(group))


LOW_ROWS = 48


class Ring:
    def __init__(self, own, slab, part, send, recv, h_send, h_recv):
        z, x, c, y = spot()
        self.first, self.second, self.block = torus(z, x, c, y)
        self.sibling = device(z, x, 1 - c, y)
        self.own, self.slab, self.part = own, slab, part
        self.send, self.recv, self.h_send, self.h_recv = send, recv, h_send, h_recv

    def ship(self, src, dst, at, to):
        return remote(src, dst, self.send.at[at], self.recv.at[at], to)

    def one(self, way):
        at = self.block(0, 0)
        return self.ship(self.own, self.slab(at), 0 if way > 0 else 1, self.first(way))

    def one_on(self, way):
        piece = self.part(self.block(-way, 0), way)
        return self.ship(piece, piece, 2 if way > 0 else 3, self.first(way))

    def two(self, d1, way):
        at = self.block(d1, 0)
        src = self.own if d1 == 0 else self.slab(at)
        return self.ship(src, self.slab(at), 4 + 4 * d1 + (0 if way > 0 else 1), self.second(way))

    def two_on(self, d1, way):
        piece = self.part(self.block(d1, -way), way)
        return self.ship(piece, piece, 6 + 4 * d1 + (0 if way > 0 else 1), self.second(way))

    def hand(self, d1, d2):
        at = self.block(d1, d2)
        src = self.own if d1 == 0 and d2 == 0 else self.slab(at)
        k = 4 * d1 + d2
        return remote(src, self.slab(at), self.h_send.at[k], self.h_recv.at[k], self.sibling)

    def open(self):
        self.one(1).start()
        self.one(-1).start()
        self.spread(0)

    def spread(self, d1):
        self.two(d1, 1).start()
        self.two(d1, -1).start()
        self.hand(d1, 0).start()

    def near(self):
        self.one(1).wait_recv()
        self.one_on(1).start()
        self.spread(3)
        self.one(-1).wait_recv()
        self.one_on(-1).start()
        self.spread(1)

    def far(self):
        self.one_on(1).wait_recv()
        self.one_on(-1).wait_recv()
        self.spread(2)

    def turn(self, d1):
        self.two(d1, 1).wait_recv()
        self.two_on(d1, 1).start()
        self.hand(d1, 3).start()
        self.two(d1, -1).wait_recv()
        self.two_on(d1, -1).start()
        self.hand(d1, 1).start()

    def end(self, d1):
        self.two_on(d1, 1).wait_recv()
        self.two_on(d1, -1).wait_recv()
        self.hand(d1, 2).start()

    def arrive(self):
        for d1 in range(4):
            for d2 in range(4):
                self.hand(d1, d2).wait_recv()

    def close(self):
        for way in (1, -1):
            self.one(way).wait_send()
            self.one_on(way).wait_send()
            for d1 in range(4):
                self.two(d1, way).wait_send()
                self.two_on(d1, way).wait_send()
        for d1 in range(4):
            for d2 in range(4):
                self.hand(d1, d2).wait_send()

    def steps(self):
        return [
            self.near,
            lambda: self.turn(0),
            self.far,
            lambda: self.turn(3),
            lambda: self.turn(1),
            lambda: self.end(0),
            lambda: self.turn(2),
            lambda: self.end(3),
            lambda: self.end(1),
            lambda: self.end(2),
        ]


def ring_scratch():
    return [DMA((20,)), DMA((20,)), DMA((16,)), DMA((16,))]


def rope_wide(cos_block, sin_block, turn):
    place = lax.axis_index("row")
    cos_at = turn[place, 0:1, :]
    sin_at = turn[place, 1:2, :]
    cosine = cos_block[...] * cos_at - sin_block[...] * sin_at
    sine = sin_block[...] * cos_at + cos_block[...] * sin_at
    lane = lax.broadcasted_iota(jnp.int32, sine.shape, 1)
    return cosine, jnp.where(lax.rem(lane, 64) < 32, -sine, sine)


def swap_halves(v):
    lane = lax.broadcasted_iota(jnp.int32, v.shape, 1)
    return jnp.where(lax.rem(lane, 64) < 32, pltpu.roll(v, 96, 1), pltpu.roll(v, 32, 1))


def over_heads(v):
    low = half_mask(0)
    left = jnp.sum(jnp.where(low, v, 0.0), axis=1, keepdims=True)
    right = jnp.sum(jnp.where(low, 0.0, v), axis=1, keepdims=True)
    return jnp.where(low, left, right)


def head_norm(raw, cosine, sine):
    scale = lax.rsqrt(over_heads(raw * raw) + EPS)
    return (raw * cosine + swap_halves(raw) * sine) * scale, scale


def front_kernel(
    hid,
    tea,
    query_w,
    key_w,
    value_w,
    out_w,
    gate_w,
    up_w,
    down_w,
    rates,
    count,
    seg,
    gains,
    cos_block,
    sin_block,
    turn,
    hid_out,
    hid_tok,
    tea_tok,
    rates_out,
    count_out,
    weights,
    raw_out,
    q_pad,
    win_out,
    att,
    out_t,
    lse,
    starts_out,
    hid_t,
    hid_n,
    tea_t,
    rate_buf,
    shard,
    shard_sib,
    own_block,
    w_first,
    win,
    o_acc,
    l_acc,
    y_send,
    y_recv,
    s_send,
    s_recv,
    local_sem,
    k_send,
    k_recv,
    a_send,
    a_recv,
    a_hsend,
    a_hrecv,
    b_send,
    b_recv,
    b_hsend,
    b_hrecv,
    t_accs,
    t_parts,
    t_send,
    t_recv,
):
    z, x, c, y = spot()
    place = 2 * x + c
    sibling = device(z, x, 1 - c, y)
    across = [device(z, x, c, wrap(y + d)) for d in (1, 2, 3)]
    tally = Tally(count, t_accs, t_parts, t_send, t_recv)

    shard[0] = jnp.concatenate(
        [query_w[:, 256:], out_w[...], query_w[:, :256], key_w[...], value_w[...]], axis=1
    )
    shard[1] = gate_w[...]
    shard[2] = up_w[...]
    shard[3] = down_w[...]
    meet(across + tally.peers[0] + tally.peers[1] + tally.peers[2])

    ours = pl.ds(pl.multiple_of(640 * c, 128), 640)
    theirs = pl.ds(pl.multiple_of(640 * (1 - c), 128), 640)

    def rows_at(at):
        return pl.multiple_of(80 * at, 16)

    ring_a = Ring(
        own_block.at[0],
        lambda at: w_first.at[pl.ds(rows_at(at), 80), ours],
        lambda at, way: w_first.at[
            pl.ds(rows_at(at), LOW_ROWS) if way > 0 else pl.ds(pl.multiple_of(80 * at + LOW_ROWS, 16), 80 - LOW_ROWS),
            ours,
        ],
        a_send,
        a_recv,
        a_hsend,
        a_hrecv,
    )
    ring_b = Ring(
        own_block.at[pl.ds(1, 3)],
        lambda at: weights.at[pl.ds(1, 3), pl.ds(rows_at(at), 80), ours],
        lambda at, way: weights.at[
            pl.ds(1, 3),
            pl.ds(rows_at(at), LOW_ROWS) if way > 0 else pl.ds(pl.multiple_of(80 * at + LOW_ROWS, 16), 80 - LOW_ROWS),
            ours,
        ],
        b_send,
        b_recv,
        b_hsend,
        b_hrecv,
    )
    head = remote(shard.at[:, :, theirs], shard_sib, s_send, s_recv, sibling)
    head.start()
    my_feats = pl.ds(pl.multiple_of(COLS * y, 64), COLS)
    hid_r = remote(hid, hid_t.at[my_feats], y_send.at[0], y_recv.at[0], across[0])
    hid_l = remote(hid, hid_t.at[my_feats], y_send.at[1], y_recv.at[1], across[2])
    hid_r.start()
    hid_l.start()
    hid_own = pltpu.make_async_copy(hid, hid_t.at[my_feats], local_sem.at[0])
    hid_own.start()
    tea_own = pltpu.make_async_copy(
        tea.at[:, pl.ds(pl.multiple_of(TOK * y, TOK), TOK)], tea_t.at[my_feats], local_sem.at[1]
    )
    tea_own.start()

    head.wait()
    for j in range(4):
        near = shard[j, :, ours].astype(F32)
        far = shard_sib[j].astype(F32)
        upper = jnp.where(c == 0, near, far)
        lower = jnp.where(c == 0, far, near)
        own_block[j] = jnp.concatenate([upper, lower], axis=0).astype(BF16)
    ring_a.open()
    own_at = ring_a.block(0, 0)
    own_a = pltpu.make_async_copy(own_block.at[0], ring_a.slab(own_at), local_sem.at[2])
    own_b = pltpu.make_async_copy(own_block.at[pl.ds(1, 3)], ring_b.slab(own_at), local_sem.at[3])
    own_a.start()
    own_b.start()
    tally.start(0)
    small = []
    for d in (1, 2, 3):
        rows = pl.ds(pl.multiple_of(TOK * wrap(y + d), TOK), TOK)
        pieces = ((tea.at[:, rows], tea_t.at[my_feats]), (rates, rate_buf.at[y]))
        for k, (src, dst) in enumerate(pieces):
            at = 4 + 2 * (d - 1) + k
            copy = remote(src, dst, y_send.at[at], y_recv.at[at], across[d - 1])
            copy.start()
            small.append(copy)
    rate_buf[y] = rates[...]

    first = jnp.sum((seg[...] < 1).astype(jnp.int32), axis=1, keepdims=True)
    second = jnp.sum((seg[...] < 2).astype(jnp.int32), axis=1, keepdims=True)
    query_seg = seg[:, pl.ds(pl.multiple_of(ROWS * place, ROWS), ROWS)]
    starts = jnp.where(query_seg == 0, 0, jnp.where(query_seg == 1, first, second))
    starts_out[...] = starts - (place - 4) * ROWS
    o_acc[...] = jnp.zeros_like(o_acc)
    l_acc[...] = jnp.zeros_like(l_acc)

    ring_a.near()
    ring_a.turn(0)
    ring_a.far()
    hid_r.wait_recv()
    hid_f_ref = hid_t.at[pl.ds(pl.multiple_of(COLS * wrap(y - 1), 64), 160)]
    hid_f = remote(hid_f_ref, hid_f_ref, y_send.at[2], y_recv.at[2], across[0])
    hid_f.start()
    hid_l.wait_recv()
    hid_g_ref = hid_t.at[pl.ds(pl.multiple_of(COLS * wrap(y + 1) + 160, 32), 160)]
    hid_g = remote(hid_g_ref, hid_g_ref, y_send.at[3], y_recv.at[3], across[2])
    hid_g.start()
    ring_a.turn(3)
    ring_a.turn(1)
    tally.finish(0)
    tally.start(1)
    ring_a.end(0)
    ring_a.turn(2)
    ring_a.end(3)
    ring_a.end(1)
    ring_a.end(2)
    tally.finish(1)
    tally.start(2)
    hid_own.wait()
    hid_f.wait_recv()
    hid_g.wait_recv()
    hid_save = pltpu.make_async_copy(hid_t, hid_out, local_sem.at[4])
    hid_save.start()
    for g in range(10):
        hid_n[:, 128 * g : 128 * g + 128] = hid_t[128 * g : 128 * g + 128, :].T
    own_a.wait()
    own_b.wait()
    ring_a.arrive()
    ring_b.open()
    w_save = pltpu.make_async_copy(w_first, weights.at[0], local_sem.at[5])
    w_save.start()

    cosine, sine = rope_wide(cos_block, sin_block, turn)
    raw = dot_nn(hid_n[...], w_first[:, 640:1280])
    for g in range(3):
        group = raw[:, 128 * g : 128 * g + 128]
        raw_out[3 + g] = group
        normed, _ = head_norm(group, cosine, sine)
        keys = normed * gains[:, 128 * g : 128 * g + 128]
        if g == 2:
            keys = jnp.where(half_mask(0), keys, group)
        win[4 * ROWS :, 128 * g : 128 * g + 128] = keys.astype(BF16)
    win[4 * ROWS :, 384:640] = raw[:, 384:640].astype(BF16)

    def slot(s):
        return win.at[pl.ds(pl.multiple_of(ROWS * s, ROWS), ROWS)]

    one = remote(slot(4), slot(2), k_send.at[0], k_recv.at[0], device(z, wrap(x + 1), c, y))
    two = remote(slot(4), slot(0), k_send.at[1], k_recv.at[1], device(z, wrap(x + 2), c, y))
    own = remote(slot(4), slot(3), k_send.at[2], k_recv.at[2], sibling)
    one_on = remote(slot(2), slot(1 + 2 * c), k_send.at[3], k_recv.at[3], sibling)
    two_on = remote(slot(0), slot(1), k_send.at[4], k_recv.at[4], sibling)

    @pl.when(x < 3)
    def _():
        one.start()

    @pl.when(x < 2)
    def _():
        two.start()

    @pl.when(c == 0)
    def _():
        own.start()

    root = math.sqrt(HEAD_DIM)
    for g, at in enumerate((384, 512, 0)):
        group = dot_nn(hid_n[...], w_first[:, at : at + 128])
        raw_out[g] = group
        normed, _ = head_norm(group, cosine, sine)
        scaled = (normed * gains[:, 128 * g : 128 * g + 128]).astype(BF16) * jnp.asarray(root, BF16)
        for half in range(2 if g < 2 else 1):
            q_pad[2 * g + half] = jnp.where(half_mask(half), scaled, jnp.zeros_like(scaled))
    hid_tok[...] = hid_n[pl.ds(pl.multiple_of(TOK * y, TOK), TOK), :]

    def tile(t):
        rows = pl.ds(pl.multiple_of(t * TILE, TILE), TILE)
        key_at = t * TILE + lax.broadcasted_iota(jnp.int32, (TILE, ROWS), 0)
        query_at = 4 * ROWS + lax.broadcasted_iota(jnp.int32, (TILE, ROWS), 1)
        allowed = (key_at >= starts_out[...]) & (key_at <= query_at)
        for h in range(HEADS):
            kg, _ = key_place(h)
            vg, vh = value_place(h)
            keys = win[rows, 128 * kg : 128 * kg + 128]
            values = win[rows, 128 * vg : 128 * vg + 128]
            scores = dot_nt(keys, q_pad[h])
            probs = jnp.where(allowed, jnp.exp(scores), 0.0)
            l_acc[h] += jnp.sum(probs.reshape(TILE // 8, 8, ROWS), axis=0)
            both = dot_tn(values, probs.astype(BF16))
            o_acc[h] += both[64 * vh : 64 * vh + 64, :]

    events = ring_b.steps()

    def step(i, carry):
        k = lax.div(i, 2)
        turned = k - 1 + 2 * lax.rem(k, 2)
        s = jnp.where(k == 0, 4, jnp.where(c == 1, 4 - k, 4 - turned))

        @pl.when((i == 2) & (c == 1))
        def _():
            own.wait_recv()

        @pl.when((x > 0) & (((i == 4) & (c == 1)) | ((i == 2) & (c == 0))))
        def _():
            one.wait_recv()
            one_on.start()

        @pl.when((x > 0) & (((i == 6) & (c == 1)) | ((i == 4) & (c == 0))))
        def _():
            one_on.wait_recv()

        @pl.when((x > 1) & (((i == 8) & (c == 1)) | ((i == 6) & (c == 0))))
        def _():
            two.wait_recv()

            @pl.when(c == 1)
            def _():
                two_on.start()

        @pl.when((x > 1) & (i == 8) & (c == 0))
        def _():
            two_on.wait_recv()

        for n, event in enumerate(events):

            @pl.when(i == n)
            def _(event=event):
                event()

        @pl.when(place + s >= 4)
        def _():
            tile(2 * s + lax.rem(i, 2))

        return carry

    lax.fori_loop(0, 10, step, 0)
    win_save = pltpu.make_async_copy(win, win_out, local_sem.at[6])
    win_save.start()
    for copy in small:
        copy.wait_recv()
    tea_own.wait()
    for g in range(10):
        tea_tok[:, 128 * g : 128 * g + 128] = tea_t[128 * g : 128 * g + 128, :].T
    rates_out[...] = jnp.concatenate([rate_buf[k] for k in range(4)], axis=1)
    tally.finish(2)
    count_out[...] = t_accs[2]
    for h in range(HEADS):
        total = jnp.sum(l_acc[h], axis=0, keepdims=True)
        lse[h] = jnp.broadcast_to(jnp.log(total), (8, ROWS))
        out_t[64 * h : 64 * h + 64, :] = o_acc[h] / total
    wide = jnp.concatenate([jnp.zeros((64, ROWS), F32), out_t[...]], axis=0)
    att[...] = wide.T.astype(BF16)
    ring_b.arrive()
    ring_a.close()
    ring_b.close()
    hid_save.wait()
    w_save.wait()
    win_save.wait()
    for copy in small + [hid_r, hid_l, hid_f, hid_g]:
        copy.wait_send()

    @pl.when(x < 3)
    def _():
        one.wait_send()

    @pl.when(x < 2)
    def _():
        two.wait_send()

    @pl.when(c == 0)
    def _():
        own.wait_send()

    @pl.when(x > 0)
    def _():
        one_on.wait_send()

    @pl.when((x > 1) & (c == 1))
    def _():
        two_on.wait_send()

    tally.close()


def rope_constants():
    inverse = np.exp(np.arange(32) * (-2.0 * math.log(10000.0) / HEAD_DIM))
    inverse = np.tile(inverse, 4)
    inside = np.arange(ROWS)[:, None] * inverse[None, :]
    at = (ROWS * np.arange(8))[:, None] * inverse[None, :]
    turn = np.stack([np.cos(at), np.sin(at)], axis=1)
    return [jnp.asarray(v, F32) for v in (np.cos(inside), np.sin(inside), turn)]


def front(hidden, teacher, shards, rates, count, segments, gains, ropes):
    sds = jax.ShapeDtypeStruct
    outs = [
        (sds((D, ROWS), BF16), IN_PLACE),
        (sds((TOK, D), BF16), IN_VMEM),
        (sds((TOK, D), BF16), IN_VMEM),
        (sds((2, D), F32), IN_VMEM),
        (sds((8, 128), F32), IN_VMEM),
        (sds((4, D, D), BF16), IN_PLACE),
        (sds((6, ROWS, 128), F32), IN_VMEM),
        (sds((HEADS, ROWS, 128), BF16), IN_VMEM),
        (sds((5 * ROWS, 2 * COLS), BF16), IN_PLACE),
        (sds((ROWS, 384), BF16), IN_VMEM),
        (sds((COLS, ROWS), F32), IN_VMEM),
        (sds((HEADS, 8, ROWS), F32), IN_VMEM),
        (sds((1, ROWS), jnp.int32), IN_VMEM),
    ]
    return pl.pallas_call(
        front_kernel,
        out_shape=tuple(o[0] for o in outs),
        in_specs=[IN_PLACE] * 2 + [IN_VMEM] * 14,
        out_specs=tuple(o[1] for o in outs),
        scratch_shapes=[
            VMEM((D, ROWS), BF16),
            VMEM((ROWS, D), BF16),
            VMEM((D, TOK), BF16),
            VMEM((4, 2, COLS), F32),
            VMEM((4, 40, D), BF16),
            VMEM((4, 40, 640), BF16),
            VMEM((4, 80, 640), BF16),
            VMEM((D, D), BF16),
            VMEM((5 * ROWS, 2 * COLS), BF16),
            VMEM((HEADS, 64, ROWS), F32),
            VMEM((HEADS, 8, ROWS), F32),
            DMA((10,)),
            DMA((10,)),
            DMA,
            DMA,
            DMA((7,)),
            DMA((5,)),
            DMA((5,)),
        ]
        + ring_scratch()
        + ring_scratch()
        + tally_scratch((8, 128)),
        compiler_params=params(0),
        name="front",
    )(hidden, teacher, *shards, rates, count, segments, gains, *ropes)


def mix_forward(states, branch, alphas):
    branch_scale = lax.rsqrt(jnp.sum(branch * branch, axis=1, keepdims=True) + EPS)
    normed = branch * branch_scale
    mixed = states + alphas * (normed - states)
    mixed_scale = lax.rsqrt(jnp.sum(mixed * mixed, axis=1, keepdims=True) + EPS)
    return mixed * mixed_scale, normed, branch_scale, mixed_scale


def mix_backward(gradient, states, normed, branch_scale, mixed_out, mixed_scale, alphas):
    along = jnp.sum(mixed_out * gradient, axis=1, keepdims=True)
    mixed_grad = mixed_scale * (gradient - mixed_out * along)
    normed_grad = alphas * mixed_grad
    toward = jnp.sum(normed * normed_grad, axis=1, keepdims=True)
    branch_grad = branch_scale * (normed_grad - normed * toward)
    rate_grad = jnp.sum(mixed_grad * (normed - states), axis=0, keepdims=True)
    return (1.0 - alphas) * mixed_grad, branch_grad, rate_grad


def swiglu_parts(gate_raw, up_raw, gate_gain, up_gain):
    root = math.sqrt(D)
    g = gate_gain * gate_raw * root
    q = jax.nn.sigmoid(g)
    return g, q


def middle_kernel(
    att,
    hid_tok,
    tea,
    mask,
    count,
    rates,
    up_gain,
    gate_gain,
    weights,
    output,
    in_one,
    product,
    mlp_grad,
    gate_low,
    up_low,
    attn_grad,
    d_att,
    res_zero,
    small,
    w_out,
    w_gate,
    w_up,
    w_down,
    raw_gate,
    raw_up,
    send_buf,
    got_buf,
    own_part,
    out_buf,
    state,
    normed,
    scales,
    w_sem,
    ag_send,
    ag_recv,
    rs_send,
    rs_recv,
    o_send,
    o_recv,
):
    z, x, c, y = spot()
    peers = [device(z, x, c, wrap(y + d)) for d in range(4)]
    loads = [
        pltpu.make_async_copy(weights.at[0, :, pl.ds(0, 384)], w_out, w_sem.at[0]),
        pltpu.make_async_copy(weights.at[1], w_gate, w_sem.at[1]),
        pltpu.make_async_copy(weights.at[2], w_up, w_sem.at[2]),
        pltpu.make_async_copy(weights.at[3], w_down, w_sem.at[3]),
    ]
    for load in loads:
        load.start()
    meet(peers[1:])
    my_rows = pl.ds(pl.multiple_of(TOK * y, TOK), TOK)

    def rows_of(k):
        return pl.ds(pl.multiple_of(TOK * wrap(y - k), TOK), TOK)

    def feats(k):
        return pl.ds(pl.multiple_of(COLS * k, 64), COLS)

    def back_to(k):
        return device(z, x, c, wrap(y - k))

    def scatter(stage, k):
        return remote(
            send_buf.at[stage, k],
            got_buf.at[stage, k],
            rs_send.at[stage, k],
            rs_recv.at[stage, k],
            back_to(k),
        )

    def spread(stage, src, k):
        return remote(
            src.at[my_rows],
            src.at[my_rows],
            ag_send.at[stage, k],
            ag_recv.at[stage, k],
            device(z, x, c, wrap(y + k)),
        )

    def give(stage, k, part):
        @pl.when(k == 0)
        def _():
            own_part[...] = part

        @pl.when(k > 0)
        def _():
            send_buf[stage, k] = part.astype(BF16)
            scatter(stage, k).start()

    def collect(stage):
        total = own_part[...]
        for k in (1, 2, 3):
            scatter(stage, k).wait_recv()
            total = total + got_buf[stage, k].astype(F32)
        return total

    def announce(stage, ref, value):
        ref[my_rows, :] = value.astype(BF16)
        for k in (2, 1, 3):
            spread(stage, ref, k).start()

    def each(body, stage=None, ref=None):
        def step(k, carry):
            if ref is not None:

                @pl.when(k > 0)
                def _():
                    spread(stage, ref, k).wait_recv()

            body(k)
            return carry

        lax.fori_loop(0, 4, step, 0)

    loads[0].wait()

    def project(k):
        give(0, k, dot_nt(att[rows_of(k), :], w_out[...]))

    each(project)
    attn = collect(0)
    states = hid_tok[...].astype(F32)
    one, normed_one, branch_one, scale_one = mix_forward(states, attn, rates[0:1, :])
    announce(0, in_one, one)
    state[0] = one
    normed[0] = normed_one
    scales[0] = jnp.broadcast_to(branch_one, (TOK, 128))
    scales[1] = jnp.broadcast_to(scale_one, (TOK, 128))
    for load in loads[1:]:
        load.wait()

    def feed(k):
        rows = rows_of(k)
        block = in_one[rows, :]
        gate_raw = dot_nn(block, w_gate[...])
        raw_gate[rows, :] = gate_raw
        up_raw = dot_nn(block, w_up[...])
        raw_up[rows, :] = up_raw
        g, q = swiglu_parts(gate_raw, up_raw, gate_gain[...], up_gain[...])
        low = (up_gain[...] * up_raw * (g * q)).astype(BF16)
        product[rows, :] = low
        give(1, k, dot_nt(low, w_down[...]))

    each(feed, 0, in_one)
    mlp = collect(1)
    one = state[0]
    two, normed_two, branch_two, scale_two = mix_forward(one, mlp, rates[1:2, :])
    for g in range(10):
        out_buf[128 * g : 128 * g + 128, :] = two[:, 128 * g : 128 * g + 128].T.astype(BF16)
    out_copies = []
    for k in (1, 2, 3):
        copy = remote(
            out_buf.at[feats(wrap(y + k))],
            output.at[:, my_rows],
            o_send.at[k],
            o_recv.at[k],
            device(z, x, c, wrap(y + k)),
        )
        out_copies.append(copy)
    errors = two - tea[...].astype(F32)
    weight = mask[...]
    loss = jnp.sum(weight * errors * errors)
    factor = 16384 * math.sqrt(D) / count[0:1, 0:1]
    seed = factor * (weight * errors)
    res_one, mlp_back, rate_two = mix_backward(
        seed, one, normed_two, branch_two, two, scale_two, rates[1:2, :]
    )
    announce(1, mlp_grad, mlp_back)
    for copy in out_copies:
        copy.start()
    output[:, my_rows] = out_buf[feats(y), :]
    small[...] = jnp.zeros_like(small)
    small[1:2, :] = rate_two
    small[4:5, :] = jnp.broadcast_to(loss, (1, D))
    state[1] = res_one

    def unfeed(k):
        rows = rows_of(k)
        grad = dot_nn(mlp_grad[rows, :], w_down[...])
        gate_raw = raw_gate[rows, :]
        up_raw = raw_up[rows, :]
        g, q = swiglu_parts(gate_raw, up_raw, gate_gain[...], up_gain[...])
        silu = g * q
        up_term = grad * silu
        slope = grad * up_gain[...] * up_raw * (q * (1.0 + g * (1.0 - q))) * math.sqrt(D)
        small[2:3, :] += jnp.sum(up_term * up_raw, axis=0, keepdims=True)
        small[3:4, :] += jnp.sum(slope * gate_raw, axis=0, keepdims=True)
        up_back = (up_term * up_gain[...]).astype(BF16)
        gate_back = (slope * gate_gain[...]).astype(BF16)
        up_low[rows, :] = up_back
        gate_low[rows, :] = gate_back
        give(2, k, dot_nt(gate_back, w_gate[...]) + dot_nt(up_back, w_up[...]))

    each(unfeed, 1, mlp_grad)
    grad_one = state[1] + collect(2)
    states = hid_tok[...].astype(F32)
    res, attn_back, rate_one = mix_backward(
        grad_one,
        states,
        normed[0],
        scales[0, :, 0:1],
        state[0],
        scales[1, :, 0:1],
        rates[0:1, :],
    )
    announce(2, attn_grad, attn_back)
    small[0:1, :] = rate_one
    for g in range(10):
        res_zero[128 * g : 128 * g + 128, :] = res[:, 128 * g : 128 * g + 128].T

    def unproject(k):
        rows = rows_of(k)
        d_att[rows, :] = dot_nn(attn_grad[rows, :], w_out[...]).astype(BF16)

    each(unproject, 2, attn_grad)
    for k in (1, 2, 3):
        for stage in range(3):
            scatter(stage, k).wait_send()
        spread(0, in_one, k).wait_send()
        spread(1, mlp_grad, k).wait_send()
        spread(2, attn_grad, k).wait_send()
    for copy in out_copies:
        copy.wait()


def middle(att, hid_tok, tea, mask, count, rates, up_gain, gate_gain, weights):
    wide = jax.ShapeDtypeStruct((ROWS, D), BF16)
    return pl.pallas_call(
        middle_kernel,
        out_shape=(
            jax.ShapeDtypeStruct((COLS, ROWS), BF16),
            wide,
            wide,
            wide,
            wide,
            wide,
            wide,
            jax.ShapeDtypeStruct((ROWS, 384), BF16),
            jax.ShapeDtypeStruct((D, TOK), F32),
            jax.ShapeDtypeStruct((8, D), F32),
        ),
        in_specs=[IN_VMEM] * 8 + [IN_PLACE],
        out_specs=(IN_VMEM,) * 10,
        scratch_shapes=[
            VMEM((D, 384), BF16),
            VMEM((D, D), BF16),
            VMEM((D, D), BF16),
            VMEM((D, D), BF16),
            VMEM((ROWS, D), F32),
            VMEM((ROWS, D), F32),
            VMEM((3, 4, TOK, D), BF16),
            VMEM((3, 4, TOK, D), BF16),
            VMEM((TOK, D), F32),
            VMEM((D, TOK), BF16),
            VMEM((2, TOK, D), F32),
            VMEM((1, TOK, D), F32),
            VMEM((2, TOK, 128), F32),
            DMA((4,)),
            DMA((3, 4)),
            DMA((3, 4)),
            DMA((3, 4)),
            DMA((3, 4)),
            DMA((4,)),
            DMA((4,)),
        ],
        compiler_params=params(3),
        name="middle",
    )(att, hid_tok, tea, mask, count, rates, up_gain, gate_gain, weights)


class Fold:
    def __init__(self, bufs, sems):
        z, x, c, y = spot()
        self.z, self.x, self.c = z, x, c
        self.first, self.second, _ = torus(z, x, c, y)
        self.at_first = x * (1 - c) + z * c
        self.sibling = device(z, x, 1 - c, y)
        self.own, self.sib, self.got_two, self.mid, self.got_one, self.fin = bufs
        self.l_sem, self.h_send, self.h_recv, self.b_send, self.b_recv, self.a_send, self.a_recv, self.f_send, self.f_recv = sems
        self.count = self.own.shape[0]
        self.lanes = pl.ds(pl.multiple_of(640 * c, 128), 640)
        self.other = pl.ds(pl.multiple_of(640 * (1 - c), 128), 640)

    def handed(self, j, d, src):
        return remote(src, self.sib.at[j, d], self.h_send.at[j, d], self.h_recv.at[j, d], self.sibling)

    def fetched(self, j, d, src):
        return pltpu.make_async_copy(src, self.own.at[j, d], self.l_sem.at[j, d])

    def open(self, srcs):
        z, x = self.z, self.x

        @pl.when(self.c == 0)
        def _():
            for d in (2, 1, 3, 0):
                for j, src in enumerate(srcs):
                    self.handed(j, d, src.at[:, wrap(x + d), :, self.other]).start()
                    self.fetched(j, d, src.at[wrap(z + d), :, :, self.lanes]).start()

        @pl.when(self.c == 1)
        def _():
            for d in (2, 1, 3, 0):
                for j, src in enumerate(srcs):
                    self.handed(j, d, src.at[wrap(z + d), :, :, self.other]).start()
                    self.fetched(j, d, src.at[:, wrap(x + d), :, self.lanes]).start()

    def pair(self, d):
        return remote(
            self.own.at[:, d], self.got_two.at[:, d - 1], self.b_send.at[d], self.b_recv.at[d], self.second(d)
        )

    def last(self, e):
        return remote(
            self.mid.at[:, e - 1], self.got_one.at[:, e - 1], self.a_send.at[e], self.a_recv.at[e], self.first(e)
        )

    def add(self, d):
        for j in range(self.count):
            blank = self.sib.at[j, d]
            self.fetched(j, d, blank).wait()
            self.handed(j, d, blank).wait_recv()

        def each(i, carry):
            j, a = lax.div(i, 4), lax.rem(i, 4)
            total = self.own[j, d, a].astype(F32) + self.sib[j, d, a].astype(F32)
            self.own[j, d, a] = total.astype(BF16)
            return carry

        lax.fori_loop(0, 4 * self.count, each, 0)
        if d:
            self.pair(d).start()

    def whole(self, j, at):
        total = self.own[j, 0, at].astype(F32)
        for d in (1, 2, 3):
            total = total + self.got_two[j, d - 1, at].astype(F32)
        return total

    def cross(self):
        for d in (1, 2, 3):
            self.pair(d).wait_recv()
        for e in (2, 1, 3):

            def each(j, carry, e=e):
                self.mid[j, e - 1] = self.whole(j, wrap(self.at_first + e)).astype(BF16)
                return carry

            lax.fori_loop(0, self.count, each, 0)
            self.last(e).start()

    def give(self, out):
        rows = pl.ds(pl.multiple_of(40 * (1 - self.c), 8), 40)
        return remote(self.fin.at[:, rows], out.at[:, :, self.lanes], self.f_send, self.f_recv, self.sibling)

    def finish(self, out):
        for e in (1, 2, 3):
            self.last(e).wait_recv()

        def each(j, carry):
            total = self.whole(j, self.at_first)
            for e in (1, 2, 3):
                total = total + self.got_one[j, e - 1].astype(F32)
            self.fin[j] = total
            return carry

        lax.fori_loop(0, self.count, each, 0)
        self.give(out).start()
        rows = pl.ds(pl.multiple_of(40 * self.c, 8), 40)
        for j in range(self.count):
            out[j, :, self.lanes] = self.fin[j, rows, :]

    def close(self, out):
        self.give(out).wait()
        for d in (1, 2, 3):
            self.pair(d).wait_send()
            self.last(d).wait_send()
        for j in range(self.count):
            for d in range(4):
                self.handed(j, d, self.sib.at[j, d]).wait_send()


def fold_scratch(count):
    block = (80, 640)
    return [
        VMEM((count, 4, 4) + block, BF16),
        VMEM((count, 4, 4) + block, BF16),
        VMEM((count, 3, 4) + block, BF16),
        VMEM((count, 3) + block, BF16),
        VMEM((count, 3) + block, BF16),
        VMEM((count,) + block, F32),
        DMA((count, 4)),
        DMA((count, 4)),
        DMA((count, 4)),
        DMA((4,)),
        DMA((4,)),
        DMA((4,)),
        DMA((4,)),
        DMA,
        DMA,
    ]


def head_back(grad, raw, gain, cosine, sine):
    normed, scale = head_norm(raw, cosine, sine)
    gain_grad = jnp.sum(grad * normed, axis=0, keepdims=True)
    pulled = grad * gain
    turned = scale * (pulled - normed * over_heads(normed * pulled))
    return turned * cosine + swap_halves(turned * sine), gain_grad


def tail_kernel(
    starts,
    q_pad,
    out_t,
    lse,
    d_att,
    att,
    gains,
    cos_block,
    sin_block,
    turn,
    res_t,
    small,
    count,
    win_in,
    raw_in,
    hid_in,
    w_in,
    attn_in,
    m0,
    m1,
    m2,
    hidden_grad,
    query_g,
    key_g,
    value_g,
    out_g,
    gate_g,
    up_g,
    down_g,
    loss_out,
    attention_out,
    feedforward_out,
    score_out,
    up_out,
    gate_out,
    win,
    raw,
    hid_t,
    w_first,
    attn,
    d_pad,
    delta,
    q_acc,
    d_win,
    sib_one,
    sib_two,
    sib_own,
    one_buf,
    two_buf,
    got_one,
    got_two,
    kv_sum,
    pack,
    out_part,
    first_g,
    y_send_buf,
    y_got_buf,
    side_src,
    side_got,
    sums,
    m_out,
    f_out,
    in_sem,
    k_send,
    k_recv,
    y_send,
    y_recv,
    v_send,
    v_recv,
    *rest,
):
    m_bufs, m_sems, rest = rest[:6], rest[6:15], rest[15:]
    f_bufs, f_sems, rest = rest[:6], rest[6:15], rest[15:]
    t_accs, t_parts, t_send, t_recv = rest
    z, x, c, y = spot()
    place = 2 * x + c
    sibling = device(z, x, 1 - c, y)
    across = [device(z, x, c, wrap(y + d)) for d in (1, 2, 3)]
    tally = Tally(sums, t_accs, t_parts, t_send, t_recv)

    def slot(ref, s):
        return ref.at[pl.ds(pl.multiple_of(ROWS * s, ROWS), ROWS)]

    win_loads = [
        pltpu.make_async_copy(slot(win_in, s), slot(win, s), in_sem.at[s]) for s in range(5)
    ]
    for s in range(5):
        win_loads[s].start()
    loads = [
        pltpu.make_async_copy(src, dst, in_sem.at[5 + k])
        for k, (src, dst) in enumerate(
            ((raw_in, raw), (attn_in, attn), (w_in.at[0], w_first), (hid_in, hid_t))
        )
    ]
    meet(across + tally.peers[0] + tally.peers[1] + tally.peers[2])
    fold_m = Fold(m_bufs, m_sems)
    fold_f = Fold(f_bufs, f_sems)
    fold_m.open([m0, m1, m2])
    side_src[...] = jnp.zeros_like(side_src)
    for k in range(4):
        lanes = slice(COLS * k, COLS * (k + 1))
        side_src[k, 0:2, 0:COLS] = small[0:2, lanes]
        side_src[k, 2:3, 0:COLS] = small[4:5, lanes]

    def side(k):
        return remote(side_src.at[wrap(y + k)], side_got.at[k], v_send.at[k], v_recv.at[k], across[k - 1])

    for k in (1, 2, 3):
        side(k).start()
    for load in loads:
        load.start()

    for h in range(HEADS):
        d_pad[h] = pad_head(d_att, (h + 1) // 2, (h + 1) % 2)
    wide = d_att[...].astype(F32).T[64:, :] * out_t[...]
    for h in range(HEADS):
        delta[h] = jnp.broadcast_to(
            jnp.sum(wide[64 * h : 64 * (h + 1), :], axis=0, keepdims=True), (8, ROWS)
        )
    q_acc[...] = jnp.zeros_like(q_acc)

    hand_one = remote(slot(d_win, 3 - 2 * c), sib_one, k_send.at[0], k_recv.at[0], sibling)
    hand_two = remote(slot(d_win, 1), sib_two, k_send.at[1], k_recv.at[1], sibling)
    hand_own = remote(slot(d_win, 3), sib_own, k_send.at[2], k_recv.at[2], sibling)
    one = remote(one_buf, got_one, k_send.at[3], k_recv.at[3], device(z, wrap(x + 3), c, y))
    two = remote(two_buf, got_two, k_send.at[4], k_recv.at[4], device(z, wrap(x + 2), c, y))

    def tile(t):
        rows = pl.ds(pl.multiple_of(t * TILE, TILE), TILE)
        key_at = t * TILE + lax.broadcasted_iota(jnp.int32, (TILE, ROWS), 0)
        query_at = 4 * ROWS + lax.broadcasted_iota(jnp.int32, (TILE, ROWS), 1)
        allowed = (key_at >= starts[...]) & (key_at <= query_at)
        terms = [None] * 5
        for h in range(HEADS):
            kg, kh = key_place(h)
            vg, _ = value_place(h)
            keys = win[rows, 128 * kg : 128 * kg + 128]
            values = win[rows, 128 * vg : 128 * vg + 128]
            scores = dot_nt(keys, q_pad[h])
            probs = jnp.where(allowed, jnp.exp(scores - lse[h, 0:1, :]), 0.0)
            prob_grad = dot_nt(values, d_pad[h])
            score_grad = (probs * (prob_grad - delta[h, 0:1, :])).astype(BF16)
            v_term = dot_nn(probs.astype(BF16), d_pad[h])
            k_term = dot_nn(score_grad, q_pad[h])
            for at, term in ((kg, k_term), (vg, v_term)):
                terms[at] = term if terms[at] is None else terms[at] + term
            both = dot_tn(keys, score_grad)
            q_acc[h] += both[64 * kh : 64 * kh + 64, :]
        for g in range(5):
            d_win[rows, 128 * g : 128 * g + 128] = terms[g].astype(BF16)

    def after(k):
        if k == 0:

            @pl.when((c == 0) & (x > 1))
            def _():
                two_buf[...] = d_win[0:ROWS, :]
                two.start()

        if k == 1:

            @pl.when((c == 0) & (x > 1))
            def _():
                hand_two.start()

            @pl.when((c == 1) & (x > 0))
            def _():
                hand_one.start()

        if k == 2:

            @pl.when((c == 0) & (x > 0))
            def _():
                hand_one.start()

            @pl.when((c == 1) & (x > 1))
            def _():
                hand_two.wait_recv()
                two_buf[...] = (
                    d_win[0:ROWS, :].astype(F32) + sib_two[...].astype(F32)
                ).astype(BF16)
                two.start()

        if k == 3:

            @pl.when(x > 0)
            def _():
                hand_one.wait_recv()
                one_buf[...] = (
                    d_win[2 * ROWS : 3 * ROWS, :].astype(F32) + sib_one[...].astype(F32)
                ).astype(BF16)
                one.start()

            @pl.when(c == 1)
            def _():
                hand_own.start()

    for load in win_loads:
        load.wait()
    folds = {2: 2, 3: 1, 5: 3, 7: 0}

    def step(i, carry):
        k = lax.div(i, 2)
        s = jnp.where((c == 0) & (k == 2), 3, jnp.where((c == 0) & (k == 3), 2, k))

        @pl.when(place + s >= 4)
        def _():
            tile(2 * s + lax.rem(i, 2))

        for k in range(4):

            @pl.when(i == 2 * k + 1)
            def _(k=k):
                after(k)

        for n, d in folds.items():

            @pl.when(i == n)
            def _(d=d):
                fold_m.add(d)

        return carry

    lax.fori_loop(0, 10, step, 0)
    for load in loads:
        load.wait()
    cosine, sine = rope_wide(cos_block, sin_block, turn)
    pack[:, 128:384] = jnp.zeros((ROWS, 256), BF16)
    gain_parts = []
    wide = jnp.concatenate([q_acc[h] for h in range(HEADS)] + [jnp.zeros((64, ROWS), F32)], axis=0)
    for g, at in enumerate((384, 512, 0)):
        grad = wide[128 * g : 128 * g + 128, :].T * math.sqrt(HEAD_DIM)
        term, gain_part = head_back(grad, raw[g], gains[:, 128 * g : 128 * g + 128], cosine, sine)
        if g == 2:
            term = jnp.where(half_mask(0), term, 0.0)
        pack[:, at : at + 128] = term.astype(BF16)
        gain_parts.append(gain_part)
    out_part[...] = dot_tn(attn[...], att[...])

    kv_sum[...] = d_win[4 * ROWS :, :].astype(F32)

    @pl.when(c == 0)
    def _():
        hand_own.wait_recv()
        kv_sum[...] += sib_own[...].astype(F32)

    @pl.when(x < 3)
    def _():
        one.wait_recv()
        kv_sum[...] += got_one[...].astype(F32)

    @pl.when(x < 2)
    def _():
        two.wait_recv()
        kv_sum[...] += got_two[...].astype(F32)

    for g in range(3):
        grad = kv_sum[:, 128 * g : 128 * g + 128]
        gain = gains[:, 128 * g : 128 * g + 128]
        term, gain_part = head_back(grad, raw[3 + g], gain, cosine, sine)
        if g == 2:
            term = jnp.where(half_mask(0), term, grad)
        at = 640 + 128 * g
        pack[:, at : at + 128] = term.astype(BF16)
        gain_parts[g] += gain_part
    pack[:, 1024:1280] = kv_sum[:, 384:640].astype(BF16)

    my_cols = pl.ds(pl.multiple_of(TOK * y, TOK), TOK)

    def project(to):
        rows = pl.ds(pl.multiple_of(COLS * to, 64), COLS)
        hidden_grad[...] = dot_nt(w_first[rows, :], pack[...])
        hidden_grad[:, my_cols] += res_t[rows, :]

    def grad_copy(k):
        return remote(y_send_buf.at[k - 1], y_got_buf.at[k - 1], y_send.at[k], y_recv.at[k], across[k - 1])

    for k in (2, 1, 3):
        project(wrap(y + k))
        y_send_buf[k - 1] = hidden_grad[...].astype(BF16)
        grad_copy(k).start()

    extra = side_src[y]
    for k in (1, 2, 3):
        side(k).wait_recv()
        extra = extra + side_got[k]
    sums[...] = jnp.zeros_like(sums)
    sums[0:2, :] = small[2:4, :]
    sums[2:3, 0:384] = jnp.concatenate(gain_parts, axis=1)
    sums[3:6, 0:384] = extra[0:3, :]
    tally.start(0)

    def first_grad(k, carry):
        rows = pl.ds(pl.multiple_of(COLS * k, 64), COLS)
        grad = dot_nn(hid_t[rows, :], pack[...])
        low = grad[:, 0:384] + out_part[rows, :]
        for a in range(4):
            first_g[k, a, :, 0:384] = low[80 * a : 80 * a + 80].astype(BF16)
            first_g[k, a, :, 384:] = grad[80 * a : 80 * a + 80, 384:].astype(BF16)
        return carry

    lax.fori_loop(0, 4, first_grad, 0)
    fold_f.open([first_g])
    fold_m.cross()
    tally.finish(0)
    tally.start(1)
    project(y)
    for d in (2, 1, 3, 0):
        fold_f.add(d)
    for k in (1, 2, 3):
        grad_copy(k).wait_recv()
        hidden_grad[...] += y_got_buf[k - 1].astype(F32)
    tally.finish(1)
    tally.start(2)
    fold_m.finish(m_out)
    fold_f.cross()
    fold_f.finish(f_out)
    tally.finish(2)
    fold_m.close(m_out)
    fold_f.close(f_out)
    gate_g[...] = m_out[0]
    up_g[...] = m_out[1]
    down_g[...] = m_out[2]
    query_g[:, 0:256] = f_out[0, :, 384:640]
    query_g[:, 256:320] = f_out[0, :, 0:64]
    key_g[...] = f_out[0, :, 640:960]
    value_g[...] = f_out[0, :, 960:1280]
    out_g[...] = f_out[0, :, 64:384]
    totals = t_accs[2]
    loss_out[...] = totals[5:6, 0:1] / count[0:1, 0:1]
    attention_out[...] = totals[3:4, 0:COLS]
    feedforward_out[...] = totals[4:5, 0:COLS]
    score_out[...] = totals[2:3, 0:COLS]
    up_out[...] = totals[0:1, :]
    gate_out[...] = totals[1:2, :]
    for k in (1, 2, 3):
        grad_copy(k).wait_send()
        side(k).wait_send()

    @pl.when(x > 0)
    def _():
        hand_one.wait_send()
        one.wait_send()

    @pl.when(x > 1)
    def _():
        two.wait_send()

        @pl.when(c == 0)
        def _():
            hand_two.wait_send()

    @pl.when(c == 1)
    def _():
        hand_own.wait_send()

    tally.close()


def tail(vmem_args, placed_args):
    sds = jax.ShapeDtypeStruct
    block = VMEM((ROWS, 2 * COLS), BF16)
    shapes = [(COLS, ROWS)] + [(40, COLS)] * 4 + [(40, D)] * 3 + [(1, 1)] + [(1, COLS)] * 3 + [(1, D)] * 2
    return pl.pallas_call(
        tail_kernel,
        out_shape=tuple(sds(s, F32) for s in shapes),
        in_specs=[IN_VMEM] * len(vmem_args) + [IN_PLACE] * len(placed_args),
        out_specs=(IN_VMEM,) * len(shapes),
        scratch_shapes=[
            VMEM((5 * ROWS, 2 * COLS), BF16),
            VMEM((6, ROWS, 128), F32),
            VMEM((D, ROWS), BF16),
            VMEM((D, D), BF16),
            VMEM((ROWS, D), BF16),
            VMEM((HEADS, ROWS, 128), BF16),
            VMEM((HEADS, 8, ROWS), F32),
            VMEM((HEADS, 64, ROWS), F32),
            VMEM((5 * ROWS, 2 * COLS), BF16),
        ]
        + [block] * 7
        + [
            VMEM((ROWS, 2 * COLS), F32),
            VMEM((ROWS, D), BF16),
            VMEM((D, 384), F32),
            VMEM((4, 4, 80, D), BF16),
            VMEM((3, COLS, ROWS), BF16),
            VMEM((3, COLS, ROWS), BF16),
            VMEM((4, 8, 384), F32),
            VMEM((4, 8, 384), F32),
            VMEM((8, D), F32),
            VMEM((3, 40, D), F32),
            VMEM((1, 40, D), F32),
            DMA((9,)),
            DMA((5,)),
            DMA((5,)),
            DMA((4,)),
            DMA((4,)),
            DMA((4,)),
            DMA((4,)),
        ]
        + fold_scratch(3)
        + fold_scratch(1)
        + tally_scratch((8, D)),
        compiler_params=params(2),
        name="tail",
    )(*vmem_args, *placed_args)


def weight_dot(inputs_low, gradient):
    return lax.dot_general(
        inputs_low, gradient, (((0,), (0,)), ((), ())), preferred_element_type=F32
    ).astype(BF16)


def shards(
    hidden,
    teacher,
    valid_mask,
    segments,
    query_weight,
    key_weight,
    value_weight,
    out_weight,
    gate_weight,
    up_weight,
    down_weight,
    attention_rate,
    feedforward_rate,
    score_gain,
    up_gain,
    gate_gain,
):
    col = lax.axis_index("col")
    token_mask = valid_mask.astype(F32)
    count = jnp.broadcast_to(jnp.sum(token_mask), (8, 128))
    rates = jnp.stack([attention_rate, feedforward_rate])
    gains = jnp.pad(score_gain, (0, 64)).reshape(1, 384)
    ropes = rope_constants()
    projections = (query_weight, key_weight, value_weight, out_weight.T)
    projections += (gate_weight, up_weight, down_weight.T)
    (
        hid_t,
        hid_tok,
        tea_tok,
        rates_full,
        count_all,
        weights,
        raw,
        q_pad,
        win,
        att,
        out_t,
        lse,
        starts,
    ) = front(hidden.T, teacher.T, projections, rates, count, segments, gains, ropes)

    mask_tok = lax.dynamic_slice_in_dim(token_mask, col * TOK, TOK).reshape(TOK, 1)
    (
        output,
        in_one,
        product,
        mlp_grad,
        gate_low,
        up_low,
        attn_grad,
        d_att,
        res_zero,
        small,
    ) = middle(
        att,
        hid_tok,
        tea_tok,
        mask_tok,
        count_all,
        rates_full,
        up_gain.reshape(1, -1),
        gate_gain.reshape(1, -1),
        weights,
    )
    gate_grad = weight_dot(in_one, gate_low)
    up_grad = weight_dot(in_one, up_low)
    down_grad = weight_dot(mlp_grad, product)

    blocks = (4, 4, 80, D)
    results = tail(
        (starts, q_pad, out_t, lse, d_att, att, gains, *ropes, res_zero, small, count_all),
        (win, raw, hid_t, weights, attn_grad)
        + tuple(g.reshape(blocks) for g in (gate_grad, up_grad, down_grad)),
    )
    hidden_grad, query_g, key_g, value_g, out_g, gate_g, up_g, down_g, loss = results[:9]
    return (
        loss.reshape(()),
        output.T,
        hidden_grad.T,
        query_g,
        key_g,
        value_g,
        out_g.T,
        gate_g,
        up_g,
        down_g.T,
    ) + tuple(v.reshape(-1) for v in results[9:])


def solution(mesh):
    both = P(("dp", "row"), "col")
    turned = P("col", ("dp", "row"))
    vector = P("col")
    in_specs = (both, both, P(("dp", "row")), P("dp", None), both, both, both, turned, both, both)
    in_specs += (turned,) + (vector,) * 5
    out_specs = (P(), both, both, both, both, both, turned, both, both, turned) + (vector,) * 5
    return jax.shard_map(shards, mesh=mesh, in_specs=in_specs, out_specs=out_specs, check_vma=False)
```

profile of v0, /device:TPU:1, one launch (start us, length us, event | category | flops | bytes accessed | tf_op | source)
XLA Modules:
  0.0 351.8 jit_solution(17222861851418250263)
XLA Ops:
  0.6 1.3 convert_reduce_fusion
  1.9 0.7 stack.9
  2.6 0.7 stack.10
  3.3 0.6 pad_maximum_fusion.rates
  3.9 0.7 pad.4
  4.6 0.6 reshape.69.gains
  5.1 0.7 convert_element_type.14
  5.8 0.1 dynamic-slice_bitcast_fusion
  5.9 1.2 broadcast_in_dim.3.count
  7.1 1.3 reshape.71.up_gain
  8.4 1.3 reshape.72.gate_gain
  9.7 0.7 copy.34.mask
  10.5 86.4 %front.1 = (bf16[1280,512]{1,0:T(8,128)(2,1)}, bf16[128,1280]{1,0:T(8,128)(2,1)}, bf16[128,1280]{1,0:T(8,128)(2,1)}, f32[2,1280]{1,0:T(2,128)}, f32[8,128]{1,0:T...) custom-call(bf16[320,512]{1,0:T(8,128)(2,1)} %bitcast.25, ...), custom_call_target="tpu_custom_call" | custom-call | tf_op jit(solution)/shard_map/front/pallas_call | solution.py:662
  96.9 110.5 %middle.1 = (bf16[320,512]{1,0:T(8,128)(2,1)}, bf16[512,1280]{1,0:T(8,128)(2,1)}, bf16[512,1280]{1,0:T(8,128)(2,1)}, bf16[512,1280]{1,0:T(8,128)(2,1)}, bf16[512...) custom-call(bf16[512,384]{1,0:T(8,128)(2,1)} %get-tuple-element.56.a, ...), custom_call_target="tpu_custom_call" | custom-call | tf_op jit(solution)/shard_map/middle/pallas_call | solution.py:949
  207.4 0.0 copy-start.10
  207.4 0.0 copy-start.11
  207.4 5.5 %convolution_convert_fusion.2 = bf16[1280,1280]{1,0:T(8,128)(2,1)} fusion(bf16[512,1280]{1,0:T(8,128)(2,1)} %get-tuple-element.69, bf16[512,1280]{1,0:T(8,128)(2,1)} %get-tuple-element.70), kind=kOutput, calls=%fused_computation.2 | convolution fusion | flops 1679360000 | bytes 5898240 | tf_op jit(solution)/shard_map/dot_general | solution.py:1542
  212.9 0.0 copy-done.10
  212.9 0.0 copy-done.11
  212.9 0.0 copy-start.9
  212.9 3.7 %convolution_convert_fusion.1 = bf16[1280,1280]{1,0:T(8,128)(2,1)} fusion(bf16[512,1280]{1,0:T(8,128)(2,1)S(1)} %copy-done.10, bf16[512,1280]{1,0:T(8,128)(2,1)S(1)} %copy-done.11), kind=kOutput, calls=%fused_computation.1 | convolution fusion | flops 1679360000 | bytes 5898240 | tf_op jit(solution)/shard_map/dot_general | solution.py:1542
  216.6 0.0 copy-done.8
  216.6 0.0 copy-done.9
  216.6 3.6 %convolution_convert_fusion = bf16[1280,1280]{1,0:T(8,128)(2,1)} fusion(bf16[512,1280]{1,0:T(8,128)(2,1)S(1)} %copy-done.9, bf16[512,1280]{1,0:T(8,128)(2,1)S(1)} %copy-done.8), kind=kOutput, calls=%fused_computation | convolution fusion | flops 1679360000 | bytes 5898240 | tf_op jit(solution)/shard_map/dot_general | solution.py:1542
  220.2 116.0 %tail.1 = (f32[320,512]{1,0:T(8,128)}, f32[40,320]{1,0:T(8,128)}, f32[40,320]{1,0:T(8,128)}, f32[40,320]{1,0:T(8,128)}, f32[40,320]{1,0:T(8,128)}, /*index=5*/f3...) custom-call(s32[1,512]{1,0:T(1,128)} %get-tuple-element.52.starts, ...), custom_call_target="tpu_custom_call" | custom-call | tf_op jit(solution)/shard_map/tail/pallas_call | solution.py:1496
  336.2 0.0 copy-start.7
  336.2 0.0 copy-start.6
  336.2 0.0 copy-start.5
  336.2 0.0 copy-start.4
  336.2 0.0 copy-start.3
  336.3 1.3 reduce
  337.6 1.3 reduce.1
  338.9 1.3 reduce.2
  340.1 1.3 reduce.3
  341.4 1.3 reduce.4
  343.4 0.0 copy-done
  343.4 0.0 copy-start.2
  343.4 0.7 copy.46
  344.1 2.0 copy.47
  346.1 0.6 copy.48
  346.8 0.0 copy-done.6
  346.8 0.6 copy.49
  347.4 0.6 copy.50
  348.0 0.6 copy.51
  348.7 0.7 copy.52
  349.3 0.7 copy.53
  350.0 0.0 copy-done.1
  350.0 0.7 copy.54
  (8 shorter events, 0.0 us)
Async XLA Ops:
  207.4 5.5 %copy-start.10 = (bf16[512,1280]{1,0:T(8,128)(2,1)S(1)}, bf16[512,1280]{1,0:T(8,128)(2,1)}, u32[]{:S(2)}) copy-start(bf16[512,1280]{1,0:T(8,128)(2,1)} %get-tuple-element.69) | copy-start | bytes 3932164
  207.4 5.5 %copy-start.11 = (bf16[512,1280]{1,0:T(8,128)(2,1)S(1)}, bf16[512,1280]{1,0:T(8,128)(2,1)}, u32[]{:S(2)}) copy-start(bf16[512,1280]{1,0:T(8,128)(2,1)} %get-tuple-element.71) | copy-start | bytes 3932164
  212.9 3.7 %copy-start.8 = (bf16[512,1280]{1,0:T(8,128)(2,1)S(1)}, bf16[512,1280]{1,0:T(8,128)(2,1)}, u32[]{:S(2)}) copy-start(bf16[512,1280]{1,0:T(8,128)(2,1)} %get-tuple-element.73) | copy-start | bytes 3932164
  212.9 3.7 %copy-start.9 = (bf16[512,1280]{1,0:T(8,128)(2,1)S(1)}, bf16[512,1280]{1,0:T(8,128)(2,1)}, u32[]{:S(2)}) copy-start(bf16[512,1280]{1,0:T(8,128)(2,1)} %get-tuple-element.72) | copy-start | bytes 3932164
  220.2 123.2 %copy-start = (bf16[320,512]{1,0:T(8,128)(2,1)S(1)}, bf16[320,512]{1,0:T(8,128)(2,1)}, u32[]{:S(2)}) copy-start(bf16[320,512]{1,0:T(8,128)(2,1)} %get-tuple-element.75) | copy-start | bytes 983044
  336.2 9.9 %copy-start.7 = (f32[40,320]{1,0:T(8,128)S(1)}, f32[40,320]{1,0:T(8,128)}, u32[]{:S(2)}) copy-start(f32[40,320]{1,0:T(8,128)} %get-tuple-element.107) | copy-start | bytes 153604
  336.2 10.6 %copy-start.6 = (f32[40,320]{1,0:T(8,128)S(1)}, f32[40,320]{1,0:T(8,128)}, u32[]{:S(2)}) copy-start(f32[40,320]{1,0:T(8,128)} %get-tuple-element.108) | copy-start | bytes 153604
  336.2 11.2 %copy-start.5 = (f32[40,320]{1,0:T(8,128)S(1)}, f32[40,320]{1,0:T(8,128)}, u32[]{:S(2)}) copy-start(f32[40,320]{1,0:T(8,128)} %get-tuple-element.109) | copy-start | bytes 153604
  336.2 11.8 %copy-start.4 = (f32[40,320]{1,0:T(8,128)S(1)}, f32[40,320]{1,0:T(8,128)}, u32[]{:S(2)}) copy-start(f32[40,320]{1,0:T(8,128)} %get-tuple-element.80) | copy-start | bytes 153604
  336.2 12.4 %copy-start.3 = (f32[40,1280]{1,0:T(8,128)S(1)}, f32[40,1280]{1,0:T(8,128)}, u32[]{:S(2)}) copy-start(f32[40,1280]{1,0:T(8,128)} %get-tuple-element.111) | copy-start | bytes 614404
  343.4 5.9 %copy-start.2 = (f32[40,1280]{1,0:T(8,128)S(1)}, f32[40,1280]{1,0:T(8,128)}, u32[]{:S(2)}) copy-start(f32[40,1280]{1,0:T(8,128)} %get-tuple-element.112) | copy-start | bytes 614404
  344.1 5.9 %copy-start.1 = (f32[40,1280]{1,0:T(8,128)S(1)}, f32[40,1280]{1,0:T(8,128)}, u32[]{:S(2)}) copy-start(f32[40,1280]{1,0:T(8,128)} %get-tuple-element.83) | copy-start | bytes 614404
where the time goes:
time: 352 us
  Pallas kernels  313 us (89%)
  local copies, waits for them, and re-layouts  14.6 us (4%)
  matrix products  12.8 us (4%)
  other arithmetic  9.06 us (3%)
    pallas_call x1, Pallas kernels, tail(): pl.pallas_call(tail_kernel, out_shape=tuple((sds(s, F32) for s in shapes)...  116 us
    pallas_call x1, Pallas kernels, middle(): pl.pallas_call(middle_kernel, out_shape=(jax.ShapeDtypeStruct((COLS, ROWS...  111 us
    pallas_call x1, Pallas kernels, front(): pl.pallas_call(front_kernel, out_shape=tuple((o[0] for o in outs)), in_sp...  86.4 us
    dot_general x3, matrix products, weight_dot(): lax.dot_general(inputs_low, gradient, (((0,), (0,)), ((), ())), preferred...  12.8 us
    unnamed x33, local copies, waits for them, and re-layouts  7.32 us

commit v1 on v0

--- a/solution.py
+++ b/solution.py
@@ -160,6 +160,36 @@
 LOW_ROWS = 48
 
 
+def lane_halves(c):
+    ours = pl.ds(pl.multiple_of(640 * c, 128), 640)
+    theirs = pl.ds(pl.multiple_of(640 * (1 - c), 128), 640)
+    return ours, theirs
+
+
+def lane_slab(ref, lanes):
+    return lambda at: ref.at[:, pl.ds(pl.multiple_of(80 * at, 16), 80), lanes]
+
+
+def lane_part(ref, lanes):
+    def part(at, way):
+        if way > 0:
+            rows = pl.ds(pl.multiple_of(80 * at, 16), LOW_ROWS)
+        else:
+            rows = pl.ds(pl.multiple_of(80 * at + LOW_ROWS, 16), 80 - LOW_ROWS)
+        return ref.at[:, rows, lanes]
+
+    return part
+
+
+def join_cores(c, shard, shard_sib, own_block, ours):
+    for j in range(own_block.shape[0]):
+        near = shard[j, :, ours].astype(F32)
+        far = shard_sib[j].astype(F32)
+        upper = jnp.where(c == 0, near, far)
+        lower = jnp.where(c == 0, far, near)
+        own_block[j] = jnp.concatenate([upper, lower], axis=0).astype(BF16)
+
+
 class Ring:
     def __init__(self, own, slab, part, send, recv, h_send, h_recv):
         z, x, c, y = spot()
@@ -299,13 +329,11 @@
     key_w,
     value_w,
     out_w,
-    gate_w,
-    up_w,
-    down_w,
-    rates,
-    count,
+    rate_one,
+    rate_two,
+    valid,
     seg,
-    gains,
+    score_gain,
     cos_block,
     sin_block,
     turn,
@@ -314,6 +342,8 @@
     tea_tok,
     rates_out,
     count_out,
+    mask_out,
+    gains_out,
     weights,
     raw_out,
     q_pad,
@@ -325,6 +355,9 @@
     hid_t,
     hid_n,
     tea_t,
+    rates,
+    count,
+    count_rows,
     rate_buf,
     shard,
     shard_sib,
@@ -344,10 +377,6 @@
     a_recv,
     a_hsend,
     a_hrecv,
-    b_send,
-    b_recv,
-    b_hsend,
-    b_hrecv,
     t_accs,
     t_parts,
     t_send,
@@ -362,42 +391,14 @@
     shard[0] = jnp.concatenate(
         [query_w[:, 256:], out_w[...], query_w[:, :256], key_w[...], value_w[...]], axis=1
     )
-    shard[1] = gate_w[...]
-    shard[2] = up_w[...]
-    shard[3] = down_w[...]
+    rates[0:1, :] = rate_one[...].reshape(1, COLS)
+    rates[1:2, :] = rate_two[...].reshape(1, COLS)
+    token_mask = valid[...].reshape(1, ROWS).astype(F32)
+    count[...] = jnp.broadcast_to(jnp.sum(token_mask, axis=1, keepdims=True), (8, 128))
     meet(across + tally.peers[0] + tally.peers[1] + tally.peers[2])
 
-    ours = pl.ds(pl.multiple_of(640 * c, 128), 640)
-    theirs = pl.ds(pl.multiple_of(640 * (1 - c), 128), 640)
-
-    def rows_at(at):
-        return pl.multiple_of(80 * at, 16)
-
-    ring_a = Ring(
-        own_block.at[0],
-        lambda at: w_first.at[pl.ds(rows_at(at), 80), ours],
-        lambda at, way: w_first.at[
-            pl.ds(rows_at(at), LOW_ROWS) if way > 0 else pl.ds(pl.multiple_of(80 * at + LOW_ROWS, 16), 80 - LOW_ROWS),
-            ours,
-        ],
-        a_send,
-        a_recv,
-        a_hsend,
-        a_hrecv,
-    )
-    ring_b = Ring(
-        own_block.at[pl.ds(1, 3)],
-        lambda at: weights.at[pl.ds(1, 3), pl.ds(rows_at(at), 80), ours],
-        lambda at, way: weights.at[
-            pl.ds(1, 3),
-            pl.ds(rows_at(at), LOW_ROWS) if way > 0 else pl.ds(pl.multiple_of(80 * at + LOW_ROWS, 16), 80 - LOW_ROWS),
-            ours,
-        ],
-        b_send,
-        b_recv,
-        b_hsend,
-        b_hrecv,
-    )
+    ours, theirs = lane_halves(c)
+    ring_a = Ring(own_block, lane_slab(w_first, ours), lane_part(w_first, ours), a_send, a_recv, a_hsend, a_hrecv)
     head = remote(shard.at[:, :, theirs], shard_sib, s_send, s_recv, sibling)
     head.start()
     my_feats = pl.ds(pl.multiple_of(COLS * y, 64), COLS)
@@ -413,18 +414,11 @@
     tea_own.start()
 
     head.wait()
-    for j in range(4):
-        near = shard[j, :, ours].astype(F32)
-        far = shard_sib[j].astype(F32)
-        upper = jnp.where(c == 0, near, far)
-        lower = jnp.where(c == 0, far, near)
-        own_block[j] = jnp.concatenate([upper, lower], axis=0).astype(BF16)
+    join_cores(c, shard, shard_sib, own_block, ours)
     ring_a.open()
     own_at = ring_a.block(0, 0)
-    own_a = pltpu.make_async_copy(own_block.at[0], ring_a.slab(own_at), local_sem.at[2])
-    own_b = pltpu.make_async_copy(own_block.at[pl.ds(1, 3)], ring_b.slab(own_at), local_sem.at[3])
+    own_a = pltpu.make_async_copy(own_block, ring_a.slab(own_at), local_sem.at[2])
     own_a.start()
-    own_b.start()
     tally.start(0)
     small = []
     for d in (1, 2, 3):
@@ -436,6 +430,11 @@
             copy.start()
             small.append(copy)
     rate_buf[y] = rates[...]
+    gains = jnp.concatenate([score_gain[...].reshape(1, COLS), jnp.zeros((1, 64), F32)], axis=1)
+    gains_out[...] = gains
+    token = pl.ds(pl.multiple_of(TOK * y, TOK), TOK)
+    count_rows[0:1, :] = token_mask
+    mask_out[...] = jnp.broadcast_to(count_rows[0:1, token], (TOK, TOK)).T
 
     first = jnp.sum((seg[...] < 1).astype(jnp.int32), axis=1, keepdims=True)
     second = jnp.sum((seg[...] < 2).astype(jnp.int32), axis=1, keepdims=True)
@@ -475,14 +474,12 @@
     for g in range(10):
         hid_n[:, 128 * g : 128 * g + 128] = hid_t[128 * g : 128 * g + 128, :].T
     own_a.wait()
-    own_b.wait()
     ring_a.arrive()
-    ring_b.open()
-    w_save = pltpu.make_async_copy(w_first, weights.at[0], local_sem.at[5])
+    w_save = pltpu.make_async_copy(w_first.at[0], weights, local_sem.at[5])
     w_save.start()
 
     cosine, sine = rope_wide(cos_block, sin_block, turn)
-    raw = dot_nn(hid_n[...], w_first[:, 640:1280])
+    raw = dot_nn(hid_n[...], w_first[0, :, 640:1280])
     for g in range(3):
         group = raw[:, 128 * g : 128 * g + 128]
         raw_out[3 + g] = group
@@ -516,7 +513,7 @@
 
     root = math.sqrt(HEAD_DIM)
     for g, at in enumerate((384, 512, 0)):
-        group = dot_nn(hid_n[...], w_first[:, at : at + 128])
+        group = dot_nn(hid_n[...], w_first[0, :, at : at + 128])
         raw_out[g] = group
         normed, _ = head_norm(group, cosine, sine)
         scaled = (normed * gains[:, 128 * g : 128 * g + 128]).astype(BF16) * jnp.asarray(root, BF16)
@@ -540,8 +537,6 @@
             both = dot_tn(values, probs.astype(BF16))
             o_acc[h] += both[64 * vh : 64 * vh + 64, :]
 
-    events = ring_b.steps()
-
     def step(i, carry):
         k = lax.div(i, 2)
         turned = k - 1 + 2 * lax.rem(k, 2)
@@ -571,12 +566,6 @@
         @pl.when((x > 1) & (i == 8) & (c == 0))
         def _():
             two_on.wait_recv()
-
-        for n, event in enumerate(events):
-
-            @pl.when(i == n)
-            def _(event=event):
-                event()
 
         @pl.when(place + s >= 4)
         def _():
@@ -601,9 +590,7 @@
         out_t[64 * h : 64 * h + 64, :] = o_acc[h] / total
     wide = jnp.concatenate([jnp.zeros((64, ROWS), F32), out_t[...]], axis=0)
     att[...] = wide.T.astype(BF16)
-    ring_b.arrive()
     ring_a.close()
-    ring_b.close()
     hid_save.wait()
     w_save.wait()
     win_save.wait()
@@ -642,7 +629,7 @@
     return [jnp.asarray(v, F32) for v in (np.cos(inside), np.sin(inside), turn)]
 
 
-def front(hidden, teacher, shards, rates, count, segments, gains, ropes):
+def front(hidden, teacher, others):
     sds = jax.ShapeDtypeStruct
     outs = [
         (sds((D, ROWS), BF16), IN_PLACE),
@@ -650,7 +637,9 @@
         (sds((TOK, D), BF16), IN_VMEM),
         (sds((2, D), F32), IN_VMEM),
         (sds((8, 128), F32), IN_VMEM),
-        (sds((4, D, D), BF16), IN_PLACE),
+        (sds((TOK, TOK), F32), IN_VMEM),
+        (sds((1, 384), F32), IN_VMEM),
+        (sds((D, D), BF16), IN_PLACE),
         (sds((6, ROWS, 128), F32), IN_VMEM),
         (sds((HEADS, ROWS, 128), BF16), IN_VMEM),
         (sds((5 * ROWS, 2 * COLS), BF16), IN_PLACE),
@@ -662,17 +651,20 @@
     return pl.pallas_call(
         front_kernel,
         out_shape=tuple(o[0] for o in outs),
-        in_specs=[IN_PLACE] * 2 + [IN_VMEM] * 14,
+        in_specs=[IN_PLACE] * 2 + [IN_VMEM] * len(others),
         out_specs=tuple(o[1] for o in outs),
         scratch_shapes=[
             VMEM((D, ROWS), BF16),
             VMEM((ROWS, D), BF16),
             VMEM((D, TOK), BF16),
+            VMEM((2, COLS), F32),
+            VMEM((8, 128), F32),
+            VMEM((8, ROWS), F32),
             VMEM((4, 2, COLS), F32),
-            VMEM((4, 40, D), BF16),
-            VMEM((4, 40, 640), BF16),
-            VMEM((4, 80, 640), BF16),
-            VMEM((D, D), BF16),
+            VMEM((1, 40, D), BF16),
+            VMEM((1, 40, 640), BF16),
+            VMEM((1, 80, 640), BF16),
+            VMEM((1, D, D), BF16),
             VMEM((5 * ROWS, 2 * COLS), BF16),
             VMEM((HEADS, 64, ROWS), F32),
             VMEM((HEADS, 8, ROWS), F32),
@@ -685,11 +677,10 @@
             DMA((5,)),
         ]
         + ring_scratch()
-        + ring_scratch()
         + tally_scratch((8, 128)),
         compiler_params=params(0),
         name="front",
-    )(hidden, teacher, *shards, rates, count, segments, gains, *ropes)
+    )(hidden, teacher, *others)
 
 
 def mix_forward(states, branch, alphas):
@@ -724,23 +715,31 @@
     mask,
     count,
     rates,
-    up_gain,
-    gate_gain,
+    up_gain_in,
+    gate_gain_in,
+    gate_w,
+    up_w,
+    down_w,
     weights,
     output,
+    attn_grad,
+    d_att,
+    res_zero,
+    small,
+    gate_out,
+    up_out,
+    down_out,
     in_one,
     product,
     mlp_grad,
     gate_low,
     up_low,
-    attn_grad,
-    d_att,
-    res_zero,
-    small,
     w_out,
-    w_gate,
-    w_up,
-    w_down,
+    w_all,
+    grads,
+    shard,
+    shard_sib,
+    own_block,
     raw_gate,
     raw_up,
     send_buf,
@@ -751,6 +750,13 @@
     normed,
     scales,
     w_sem,
+    g_sem,
+    s_send,
+    s_recv,
+    b_send,
+    b_recv,
+    b_hsend,
+    b_hrecv,
     ag_send,
     ag_recv,
     rs_send,
@@ -760,15 +766,24 @@
 ):
     z, x, c, y = spot()
     peers = [device(z, x, c, wrap(y + d)) for d in range(4)]
-    loads = [
-        pltpu.make_async_copy(weights.at[0, :, pl.ds(0, 384)], w_out, w_sem.at[0]),
-        pltpu.make_async_copy(weights.at[1], w_gate, w_sem.at[1]),
-        pltpu.make_async_copy(weights.at[2], w_up, w_sem.at[2]),
-        pltpu.make_async_copy(weights.at[3], w_down, w_sem.at[3]),
-    ]
-    for load in loads:
-        load.start()
-    meet(peers[1:])
+    load = pltpu.make_async_copy(weights.at[:, pl.ds(0, 384)], w_out, w_sem.at[0])
+    load.start()
+    shard[0] = gate_w[...]
+    shard[1] = up_w[...]
+    shard[2] = down_w[...]
+    up_gain = up_gain_in[...].reshape(1, D)
+    gate_gain = gate_gain_in[...].reshape(1, D)
+    w_gate, w_up, w_down = (w_all.at[k] for k in range(3))
+    sibling = device(z, x, 1 - c, y)
+    ring_peers = [device(z, wrap(x + d), c, y) for d in (1, 3)]
+    ring_peers += [device(wrap(z + d), x, c, y) for d in (1, 3)]
+    meet(peers[1:] + ring_peers + [sibling])
+    ours, theirs = lane_halves(c)
+    ring = Ring(
+        own_block, lane_slab(w_all, ours), lane_part(w_all, ours), b_send, b_recv, b_hsend, b_hrecv
+    )
+    head = remote(shard.at[:, :, theirs], shard_sib, s_send, s_recv, sibling)
+    head.start()
     my_rows = pl.ds(pl.multiple_of(TOK * y, TOK), TOK)
 
     def rows_of(k):
@@ -782,8 +797,8 @@
 
     def scatter(stage, k):
         return remote(
-            send_buf.at[stage, k],
-            got_buf.at[stage, k],
+            send_buf.at[stage, k - 1],
+            got_buf.at[stage, k - 1],
             rs_send.at[stage, k],
             rs_recv.at[stage, k],
             back_to(k),
@@ -805,14 +820,14 @@
 
         @pl.when(k > 0)
         def _():
-            send_buf[stage, k] = part.astype(BF16)
+            send_buf[stage, k - 1] = part.astype(BF16)
             scatter(stage, k).start()
 
     def collect(stage):
         total = own_part[...]
         for k in (1, 2, 3):
             scatter(stage, k).wait_recv()
-            total = total + got_buf[stage, k].astype(F32)
+            total = total + got_buf[stage, k - 1].astype(F32)
         return total
 
     def announce(stage, ref, value):
@@ -833,12 +848,19 @@
 
         lax.fori_loop(0, 4, step, 0)
 
-    loads[0].wait()
-
-    def project(k):
-        give(0, k, dot_nt(att[rows_of(k), :], w_out[...]))
-
-    each(project)
+    load.wait()
+    for k in (2, 1, 3):
+        send_buf[0, k - 1] = dot_nt(att[rows_of(k), :], w_out[...]).astype(BF16)
+        scatter(0, k).start()
+    head.wait()
+    join_cores(c, shard, shard_sib, own_block, ours)
+    ring.open()
+    ring_own = pltpu.make_async_copy(own_block, ring.slab(ring.block(0, 0)), w_sem.at[1])
+    ring_own.start()
+    own_part[...] = dot_nt(att[my_rows, :], w_out[...])
+    ring.near()
+    ring.turn(0)
+    ring.far()
     attn = collect(0)
     states = hid_tok[...].astype(F32)
     one, normed_one, branch_one, scale_one = mix_forward(states, attn, rates[0:1, :])
@@ -847,8 +869,15 @@
     normed[0] = normed_one
     scales[0] = jnp.broadcast_to(branch_one, (TOK, 128))
     scales[1] = jnp.broadcast_to(scale_one, (TOK, 128))
-    for load in loads[1:]:
-        load.wait()
+    ring.turn(3)
+    ring.turn(1)
+    ring.end(0)
+    ring.turn(2)
+    ring.end(3)
+    ring.end(1)
+    ring.end(2)
+    ring_own.wait()
+    ring.arrive()
 
     def feed(k):
         rows = rows_of(k)
@@ -857,8 +886,8 @@
         raw_gate[rows, :] = gate_raw
         up_raw = dot_nn(block, w_up[...])
         raw_up[rows, :] = up_raw
-        g, q = swiglu_parts(gate_raw, up_raw, gate_gain[...], up_gain[...])
-        low = (up_gain[...] * up_raw * (g * q)).astype(BF16)
+        g, q = swiglu_parts(gate_raw, up_raw, gate_gain, up_gain)
+        low = (up_gain * up_raw * (g * q)).astype(BF16)
         product[rows, :] = low
         give(1, k, dot_nt(low, w_down[...]))
 
@@ -879,7 +908,7 @@
         )
         out_copies.append(copy)
     errors = two - tea[...].astype(F32)
-    weight = mask[...]
+    weight = mask[:, 0:1]
     loss = jnp.sum(weight * errors * errors)
     factor = 16384 * math.sqrt(D) / count[0:1, 0:1]
     seed = factor * (weight * errors)
@@ -900,19 +929,30 @@
         grad = dot_nn(mlp_grad[rows, :], w_down[...])
         gate_raw = raw_gate[rows, :]
         up_raw = raw_up[rows, :]
-        g, q = swiglu_parts(gate_raw, up_raw, gate_gain[...], up_gain[...])
+        g, q = swiglu_parts(gate_raw, up_raw, gate_gain, up_gain)
         silu = g * q
         up_term = grad * silu
-        slope = grad * up_gain[...] * up_raw * (q * (1.0 + g * (1.0 - q))) * math.sqrt(D)
+        slope = grad * up_gain * up_raw * (q * (1.0 + g * (1.0 - q))) * math.sqrt(D)
         small[2:3, :] += jnp.sum(up_term * up_raw, axis=0, keepdims=True)
         small[3:4, :] += jnp.sum(slope * gate_raw, axis=0, keepdims=True)
-        up_back = (up_term * up_gain[...]).astype(BF16)
-        gate_back = (slope * gate_gain[...]).astype(BF16)
+        up_back = (up_term * up_gain).astype(BF16)
+        gate_back = (slope * gate_gain).astype(BF16)
         up_low[rows, :] = up_back
         gate_low[rows, :] = gate_back
         give(2, k, dot_nt(gate_back, w_gate[...]) + dot_nt(up_back, w_up[...]))
 
     each(unfeed, 1, mlp_grad)
+
+    def weight_grad(j, left, right, out):
+        def step(k, carry):
+            rows = pl.ds(pl.multiple_of(256 * k, 256), 256)
+            grads[j, rows, :] = dot_tn(left[:, rows], right[...]).astype(BF16)
+            return carry
+
+        lax.fori_loop(0, 5, step, 0)
+        pltpu.make_async_copy(grads.at[j], out, g_sem.at[j]).start()
+
+    weight_grad(2, mlp_grad, product, down_out)
     grad_one = state[1] + collect(2)
     states = hid_tok[...].astype(F32)
     res, attn_back, rate_one = mix_backward(
@@ -933,7 +973,12 @@
         rows = rows_of(k)
         d_att[rows, :] = dot_nn(attn_grad[rows, :], w_out[...]).astype(BF16)
 
+    weight_grad(0, in_one, gate_low, gate_out)
+    weight_grad(1, in_one, up_low, up_out)
     each(unproject, 2, attn_grad)
+    for j, out in enumerate((gate_out, up_out, down_out)):
+        pltpu.make_async_copy(grads.at[j], out, g_sem.at[j]).wait()
+    ring.close()
     for k in (1, 2, 3):
         for stage in range(3):
             scatter(stage, k).wait_send()
@@ -944,39 +989,52 @@
         copy.wait()
 
 
-def middle(att, hid_tok, tea, mask, count, rates, up_gain, gate_gain, weights):
-    wide = jax.ShapeDtypeStruct((ROWS, D), BF16)
+def middle(vmem_args, weights):
+    sds = jax.ShapeDtypeStruct
+    wide = VMEM((ROWS, D), BF16)
+    square = sds((D, D), BF16)
     return pl.pallas_call(
         middle_kernel,
         out_shape=(
-            jax.ShapeDtypeStruct((COLS, ROWS), BF16),
+            sds((COLS, ROWS), BF16),
+            sds((ROWS, D), BF16),
+            sds((ROWS, 384), BF16),
+            sds((D, TOK), F32),
+            sds((8, D), F32),
+            square,
+            square,
+            square,
+        ),
+        in_specs=[IN_VMEM] * len(vmem_args) + [IN_PLACE],
+        out_specs=(IN_VMEM,) * 5 + (IN_PLACE,) * 3,
+        scratch_shapes=[
             wide,
             wide,
             wide,
             wide,
             wide,
-            wide,
-            jax.ShapeDtypeStruct((ROWS, 384), BF16),
-            jax.ShapeDtypeStruct((D, TOK), F32),
-            jax.ShapeDtypeStruct((8, D), F32),
-        ),
-        in_specs=[IN_VMEM] * 8 + [IN_PLACE],
-        out_specs=(IN_VMEM,) * 10,
-        scratch_shapes=[
             VMEM((D, 384), BF16),
-            VMEM((D, D), BF16),
-            VMEM((D, D), BF16),
-            VMEM((D, D), BF16),
+            VMEM((3, D, D), BF16),
+            VMEM((3, D, D), BF16),
+            VMEM((3, 40, D), BF16),
+            VMEM((3, 40, 640), BF16),
+            VMEM((3, 80, 640), BF16),
             VMEM((ROWS, D), F32),
             VMEM((ROWS, D), F32),
-            VMEM((3, 4, TOK, D), BF16),
-            VMEM((3, 4, TOK, D), BF16),
+            VMEM((3, 3, TOK, D), BF16),
+            VMEM((3, 3, TOK, D), BF16),
             VMEM((TOK, D), F32),
             VMEM((D, TOK), BF16),
             VMEM((2, TOK, D), F32),
             VMEM((1, TOK, D), F32),
             VMEM((2, TOK, 128), F32),
-            DMA((4,)),
+            DMA((2,)),
+            DMA((3,)),
+            DMA,
+            DMA,
+        ]
+        + ring_scratch()
+        + [
             DMA((3, 4)),
             DMA((3, 4)),
             DMA((3, 4)),
@@ -984,17 +1042,23 @@
             DMA((4,)),
             DMA((4,)),
         ],
-        compiler_params=params(3),
+        compiler_params=params(1),
         name="middle",
-    )(att, hid_tok, tea, mask, count, rates, up_gain, gate_gain, weights)
+    )(*vmem_args, weights)
 
 
 class Fold:
-    def __init__(self, bufs, sems):
+    def __init__(self, bufs, sems, z_heavy):
         z, x, c, y = spot()
         self.z, self.x, self.c = z, x, c
-        self.first, self.second, _ = torus(z, x, c, y)
-        self.at_first = x * (1 - c) + z * c
+        self.z_heavy = z_heavy
+        if z_heavy:
+            self.first = lambda d: device(z, wrap(x + d), c, y)
+            self.second = lambda d: device(wrap(z + d), x, c, y)
+            self.at_first = x
+        else:
+            self.first, self.second, _ = torus(z, x, c, y)
+            self.at_first = x * (1 - c) + z * c
         self.sibling = device(z, x, 1 - c, y)
         self.own, self.sib, self.got_two, self.mid, self.got_one, self.fin = bufs
         self.l_sem, self.h_send, self.h_recv, self.b_send, self.b_recv, self.a_send, self.a_recv, self.f_send, self.f_recv = sems
@@ -1010,6 +1074,12 @@
 
     def open(self, srcs):
         z, x = self.z, self.x
+        if self.z_heavy:
+            for d in (2, 1, 3, 0):
+                for j, src in enumerate(srcs):
+                    self.handed(j, d, src.at[wrap(z + d), :, :, self.other]).start()
+                    self.fetched(j, d, src.at[wrap(z + d), :, :, self.lanes]).start()
+            return
 
         @pl.when(self.c == 0)
         def _():
@@ -1159,12 +1229,7 @@
     gate_g,
     up_g,
     down_g,
-    loss_out,
-    attention_out,
-    feedforward_out,
-    score_out,
-    up_out,
-    gate_out,
+    sums_out,
     win,
     raw,
     hid_t,
@@ -1221,12 +1286,12 @@
     loads = [
         pltpu.make_async_copy(src, dst, in_sem.at[5 + k])
         for k, (src, dst) in enumerate(
-            ((raw_in, raw), (attn_in, attn), (w_in.at[0], w_first), (hid_in, hid_t))
+            ((raw_in, raw), (attn_in, attn), (w_in, w_first), (hid_in, hid_t))
         )
     ]
     meet(across + tally.peers[0] + tally.peers[1] + tally.peers[2])
-    fold_m = Fold(m_bufs, m_sems)
-    fold_f = Fold(f_bufs, f_sems)
+    fold_m = Fold(m_bufs, m_sems, True)
+    fold_f = Fold(f_bufs, f_sems, False)
     fold_m.open([m0, m1, m2])
     side_src[...] = jnp.zeros_like(side_src)
     for k in range(4):
@@ -1458,13 +1523,8 @@
     key_g[...] = f_out[0, :, 640:960]
     value_g[...] = f_out[0, :, 960:1280]
     out_g[...] = f_out[0, :, 64:384]
-    totals = t_accs[2]
-    loss_out[...] = totals[5:6, 0:1] / count[0:1, 0:1]
-    attention_out[...] = totals[3:4, 0:COLS]
-    feedforward_out[...] = totals[4:5, 0:COLS]
-    score_out[...] = totals[2:3, 0:COLS]
-    up_out[...] = totals[0:1, :]
-    gate_out[...] = totals[1:2, :]
+    sums_out[...] = t_accs[2]
+    sums_out[6:7, :] = jnp.broadcast_to(count[0:1, 0:1], (1, D))
     for k in (1, 2, 3):
         grad_copy(k).wait_send()
         side(k).wait_send()
@@ -1492,7 +1552,7 @@
 def tail(vmem_args, placed_args):
     sds = jax.ShapeDtypeStruct
     block = VMEM((ROWS, 2 * COLS), BF16)
-    shapes = [(COLS, ROWS)] + [(40, COLS)] * 4 + [(40, D)] * 3 + [(1, 1)] + [(1, COLS)] * 3 + [(1, D)] * 2
+    shapes = [(COLS, ROWS)] + [(40, COLS)] * 4 + [(40, D)] * 3 + [(8, D)]
     return pl.pallas_call(
         tail_kernel,
         out_shape=tuple(sds(s, F32) for s in shapes),
@@ -1538,10 +1598,30 @@
     )(*vmem_args, *placed_args)
 
 
-def weight_dot(inputs_low, gradient):
-    return lax.dot_general(
-        inputs_low, gradient, (((0,), (0,)), ((), ())), preferred_element_type=F32
-    ).astype(BF16)
+def emit_kernel(sums, *refs):
+    count = (len(refs) - 6) // 2
+    for src, dst in zip(refs[:count], refs[count : 2 * count]):
+        dst[...] = src[...]
+    loss, attention, feedforward, score, up, gate = refs[2 * count :]
+    loss[0] = jnp.sum(sums[5:6, 0:1] / sums[6:7, 0:1])
+    score[...] = sums[2:3, 0:COLS].reshape(COLS)
+    attention[...] = sums[3:4, 0:COLS].reshape(COLS)
+    feedforward[...] = sums[4:5, 0:COLS].reshape(COLS)
+    up[...] = sums[0:1, :].reshape(D)
+    gate[...] = sums[1:2, :].reshape(D)
+
+
+def emit(sums, arrays):
+    sds = jax.ShapeDtypeStruct
+    vectors = [sds((1,), F32)] + [sds((COLS,), F32)] * 3 + [sds((D,), F32)] * 2
+    return pl.pallas_call(
+        emit_kernel,
+        out_shape=tuple(sds(a.shape, a.dtype) for a in arrays) + tuple(vectors),
+        in_specs=[IN_VMEM] * (1 + len(arrays)),
+        out_specs=(IN_VMEM,) * len(arrays) + (IN_SMEM,) + (IN_VMEM,) * 5,
+        compiler_params=params(),
+        name="emit",
+    )(sums, *arrays)
 
 
 def shards(
@@ -1562,20 +1642,17 @@
     up_gain,
     gate_gain,
 ):
-    col = lax.axis_index("col")
-    token_mask = valid_mask.astype(F32)
-    count = jnp.broadcast_to(jnp.sum(token_mask), (8, 128))
-    rates = jnp.stack([attention_rate, feedforward_rate])
-    gains = jnp.pad(score_gain, (0, 64)).reshape(1, 384)
     ropes = rope_constants()
-    projections = (query_weight, key_weight, value_weight, out_weight.T)
-    projections += (gate_weight, up_weight, down_weight.T)
+    others = (query_weight, key_weight, value_weight, out_weight.T)
+    others += (attention_rate, feedforward_rate, valid_mask, segments, score_gain, *ropes)
     (
         hid_t,
         hid_tok,
         tea_tok,
-        rates_full,
-        count_all,
+        rates,
+        count,
+        mask,
+        gains,
         weights,
         raw,
         q_pad,
@@ -1584,44 +1661,31 @@
         out_t,
         lse,
         starts,
-    ) = front(hidden.T, teacher.T, projections, rates, count, segments, gains, ropes)
-
-    mask_tok = lax.dynamic_slice_in_dim(token_mask, col * TOK, TOK).reshape(TOK, 1)
-    (
-        output,
-        in_one,
-        product,
-        mlp_grad,
-        gate_low,
-        up_low,
-        attn_grad,
-        d_att,
-        res_zero,
-        small,
-    ) = middle(
-        att,
-        hid_tok,
-        tea_tok,
-        mask_tok,
-        count_all,
-        rates_full,
-        up_gain.reshape(1, -1),
-        gate_gain.reshape(1, -1),
+    ) = front(hidden.T, teacher.T, others)
+    output, attn_grad, d_att, res_t, small, *grads = middle(
+        (
+            att,
+            hid_tok,
+            tea_tok,
+            mask,
+            count,
+            rates,
+            up_gain,
+            gate_gain,
+            gate_weight,
+            up_weight,
+            down_weight.T,
+        ),
         weights,
     )
-    gate_grad = weight_dot(in_one, gate_low)
-    up_grad = weight_dot(in_one, up_low)
-    down_grad = weight_dot(mlp_grad, product)
-
-    blocks = (4, 4, 80, D)
     results = tail(
-        (starts, q_pad, out_t, lse, d_att, att, gains, *ropes, res_zero, small, count_all),
-        (win, raw, hid_t, weights, attn_grad)
-        + tuple(g.reshape(blocks) for g in (gate_grad, up_grad, down_grad)),
+        (starts, q_pad, out_t, lse, d_att, att, gains, *ropes, res_t, small, count),
+        (win, raw, hid_t, weights, attn_grad) + tuple(g.reshape(4, 4, 80, D) for g in grads),
     )
-    hidden_grad, query_g, key_g, value_g, out_g, gate_g, up_g, down_g, loss = results[:9]
+    results = emit(results[8], (output,) + tuple(results[:8]))
+    output, hidden_grad, query_g, key_g, value_g, out_g, gate_g, up_g, down_g = results[:9]
     return (
-        loss.reshape(()),
+        results[9].reshape(()),
         output.T,
         hidden_grad.T,
         query_g,
@@ -1631,7 +1695,7 @@
         gate_g,
         up_g,
         down_g.T,
-    ) + tuple(v.reshape(-1) for v in results[9:])
+    ) + tuple(results[10:])
 
 
 def solution(mesh):

time: 352 us -> 293 us (0.83)
  Pallas kernels: 313 us -> 292 us
  local copies, waits for them, and re-layouts: 14.6 us -> 0 us
  matrix products: 12.8 us -> 0 us
  other arithmetic: 9.06 us -> 0 us
    pallas_call x1, Pallas kernels: 86.4 us -> 61.6 us  [front(): pl.pallas_call(front_kernel, out_shape=tuple((o[0] for o in outs)), in_sp...]
    pallas_call x1 -> x2, Pallas kernels: 111 us -> 127 us  [the longest x1 125 us: middle(): pl.pallas_call(middle_kernel, out_shape=(sds((COLS, ROWS), BF16), sds((RO...]
    pallas_call x1, Pallas kernels: 116 us -> 103 us  [tail(): pl.pallas_call(tail_kernel, out_shape=tuple((sds(s, F32) for s in shapes)...]
    dot_general x3 -> x0, matrix products: 12.8 us -> none  [weight_dot(): lax.dot_general(inputs_low, gradient, (((0,), (0,)), ((), ())), preferred...]
    unnamed x33 -> x0, local copies, waits for them, and re-layouts: 7.32 us -> none
    pallas_call x5 -> x0, other arithmetic: 6.5 us -> none  [tail(): pl.pallas_call(tail_kernel, out_shape=tuple((sds(s, F32) for s in shapes)...]
    reshape x5 -> x0, local copies, waits for them, and re-layouts: 3.97 us -> none  [the longest x1 1.29 us: shards(): up_gain.reshape(1, -1)]
where the time goes in v1:
time: 293 us
  Pallas kernels  292 us (100%)
    pallas_call x1, Pallas kernels, middle(): pl.pallas_call(middle_kernel, out_shape=(sds((COLS, ROWS), BF16), sds((RO...  125 us
    pallas_call x1, Pallas kernels, tail(): pl.pallas_call(tail_kernel, out_shape=tuple((sds(s, F32) for s in shapes)...  103 us
    pallas_call x1, Pallas kernels, front(): pl.pallas_call(front_kernel, out_shape=tuple((o[0] for o in outs)), in_sp...  61.6 us

profile of v1, /device:TPU:1, one launch (start us, length us, event | category | flops | bytes accessed | tf_op | source)
XLA Modules:
  0.0 292.7 jit_solution(3957338789767626957)
XLA Ops:
  0.6 61.6 %front.1 = (bf16[1280,512]{1,0:T(8,128)(2,1)}, bf16[128,1280]{1,0:T(8,128)(2,1)}, bf16[128,1280]{1,0:T(8,128)(2,1)}, f32[2,1280]{1,0:T(2,128)}, f32[8,128]{1,0:T...) custom-call(bf16[320,512]{1,0:T(8,128)(2,1)} %bitcast.15, ...), custom_call_target="tpu_custom_call" | custom-call | tf_op jit(solution)/shard_map/front/pallas_call | solution.py:651
  62.2 124.5 %middle.1 = (bf16[320,512]{1,0:T(8,128)(2,1)}, bf16[512,1280]{1,0:T(8,128)(2,1)}, bf16[512,384]{1,0:T(8,128)(2,1)}, f32[1280,128]{1,0:T(8,128)}, f32[8,1280]{1,0...) custom-call(bf16[512,384]{1,0:T(8,128)(2,1)} %get-tuple-element.66.att, ...), custom_call_target="tpu_custom_call" | custom-call | tf_op jit(solution)/shard_map/middle/pallas_call | solution.py:996
  186.8 102.9 %tail.1 = (f32[320,512]{1,0:T(8,128)}, f32[40,320]{1,0:T(8,128)}, f32[40,320]{1,0:T(8,128)}, f32[40,320]{1,0:T(8,128)}, f32[40,320]{1,0:T(8,128)}, /*index=5*/f3...) custom-call(s32[1,512]{1,0:T(1,128)} %get-tuple-element.62.starts, ...), custom_call_target="tpu_custom_call" | custom-call | tf_op jit(solution)/shard_map/tail/pallas_call | solution.py:1556
  289.7 2.8 emit.1

commit v2 on v1

--- a/solution.py
+++ b/solution.py
@@ -122,19 +122,21 @@
     ]
 
 
-def torus(z, x, c, y):
+def torus(z, x, c, y, z_last=False):
+    turn = 0 if z_last else c
+
     def first(d):
-        return device(wrap(z + c * d), wrap(x + (1 - c) * d), c, y)
+        return device(wrap(z + turn * d), wrap(x + (1 - turn) * d), c, y)
 
     def second(d):
-        return device(wrap(z + (1 - c) * d), wrap(x + c * d), c, y)
-
-    at_first = x * (1 - c) + z * c
-    at_second = z * (1 - c) + x * c
+        return device(wrap(z + (1 - turn) * d), wrap(x + turn * d), c, y)
+
+    at_first = x * (1 - turn) + z * turn
+    at_second = z * (1 - turn) + x * turn
 
     def block(d1, d2):
         a1, a2 = wrap(at_first + d1), wrap(at_second + d2)
-        return (1 - c) * (a2 * 4 + a1) + c * (a1 * 4 + a2)
+        return (1 - turn) * (a2 * 4 + a1) + turn * (a1 * 4 + a2)
 
     return first, second, block
 
@@ -191,9 +193,9 @@
 
 
 class Ring:
-    def __init__(self, own, slab, part, send, recv, h_send, h_recv):
+    def __init__(self, own, slab, part, send, recv, h_send, h_recv, z_last=False):
         z, x, c, y = spot()
-        self.first, self.second, self.block = torus(z, x, c, y)
+        self.first, self.second, self.block = torus(z, x, c, y, z_last)
         self.sibling = device(z, x, 1 - c, y)
         self.own, self.slab, self.part = own, slab, part
         self.send, self.recv, self.h_send, self.h_recv = send, recv, h_send, h_recv
@@ -329,6 +331,9 @@
     key_w,
     value_w,
     out_w,
+    gate_w,
+    up_w,
+    down_w,
     rate_one,
     rate_two,
     valid,
@@ -345,6 +350,7 @@
     mask_out,
     gains_out,
     weights,
+    w_rest,
     raw_out,
     q_pad,
     win_out,
@@ -362,6 +368,9 @@
     shard,
     shard_sib,
     own_block,
+    shard_b,
+    shard_b_sib,
+    own_b,
     w_first,
     win,
     o_acc,
@@ -377,6 +386,10 @@
     a_recv,
     a_hsend,
     a_hrecv,
+    b_send,
+    b_recv,
+    b_hsend,
+    b_hrecv,
     t_accs,
     t_parts,
     t_send,
@@ -391,6 +404,9 @@
     shard[0] = jnp.concatenate(
         [query_w[:, 256:], out_w[...], query_w[:, :256], key_w[...], value_w[...]], axis=1
     )
+    shard_b[0] = gate_w[...]
+    shard_b[1] = up_w[...]
+    shard_b[2] = down_w[...]
     rates[0:1, :] = rate_one[...].reshape(1, COLS)
     rates[1:2, :] = rate_two[...].reshape(1, COLS)
     token_mask = valid[...].reshape(1, ROWS).astype(F32)
@@ -399,8 +415,13 @@
 
     ours, theirs = lane_halves(c)
     ring_a = Ring(own_block, lane_slab(w_first, ours), lane_part(w_first, ours), a_send, a_recv, a_hsend, a_hrecv)
-    head = remote(shard.at[:, :, theirs], shard_sib, s_send, s_recv, sibling)
+    ring_b = Ring(
+        own_b, lane_slab(w_rest, ours), lane_part(w_rest, ours), b_send, b_recv, b_hsend, b_hrecv, True
+    )
+    head = remote(shard.at[:, :, theirs], shard_sib, s_send.at[0], s_recv.at[0], sibling)
     head.start()
+    head_b = remote(shard_b.at[:, :, theirs], shard_b_sib, s_send.at[1], s_recv.at[1], sibling)
+    head_b.start()
     my_feats = pl.ds(pl.multiple_of(COLS * y, 64), COLS)
     hid_r = remote(hid, hid_t.at[my_feats], y_send.at[0], y_recv.at[0], across[0])
     hid_l = remote(hid, hid_t.at[my_feats], y_send.at[1], y_recv.at[1], across[2])
@@ -445,8 +466,13 @@
     l_acc[...] = jnp.zeros_like(l_acc)
 
     ring_a.near()
+    head_b.wait()
+    join_cores(c, shard_b, shard_b_sib, own_b, ours)
+    own_rest = pltpu.make_async_copy(own_b, ring_b.slab(ring_b.block(0, 0)), local_sem.at[3])
+    own_rest.start()
     ring_a.turn(0)
     ring_a.far()
+    ring_b.open()
     hid_r.wait_recv()
     hid_f_ref = hid_t.at[pl.ds(pl.multiple_of(COLS * wrap(y - 1), 64), 160)]
     hid_f = remote(hid_f_ref, hid_f_ref, y_send.at[2], y_recv.at[2], across[0])
@@ -475,6 +501,7 @@
         hid_n[:, 128 * g : 128 * g + 128] = hid_t[128 * g : 128 * g + 128, :].T
     own_a.wait()
     ring_a.arrive()
+    ring_b.near()
     w_save = pltpu.make_async_copy(w_first.at[0], weights, local_sem.at[5])
     w_save.start()
 
@@ -520,6 +547,10 @@
         for half in range(2 if g < 2 else 1):
             q_pad[2 * g + half] = jnp.where(half_mask(half), scaled, jnp.zeros_like(scaled))
     hid_tok[...] = hid_n[pl.ds(pl.multiple_of(TOK * y, TOK), TOK), :]
+
+    ring_b.turn(0)
+    ring_b.far()
+    events = ring_b.steps()[3:]
 
     def tile(t):
         rows = pl.ds(pl.multiple_of(t * TILE, TILE), TILE)
@@ -566,6 +597,12 @@
         @pl.when((x > 1) & (i == 8) & (c == 0))
         def _():
             two_on.wait_recv()
+
+        for n, event in enumerate(events):
+
+            @pl.when(i == n + 2)
+            def _(event=event):
+                event()
 
         @pl.when(place + s >= 4)
         def _():
@@ -590,7 +627,10 @@
         out_t[64 * h : 64 * h + 64, :] = o_acc[h] / total
     wide = jnp.concatenate([jnp.zeros((64, ROWS), F32), out_t[...]], axis=0)
     att[...] = wide.T.astype(BF16)
+    ring_b.arrive()
+    own_rest.wait()
     ring_a.close()
+    ring_b.close()
     hid_save.wait()
     w_save.wait()
     win_save.wait()
@@ -640,6 +680,7 @@
         (sds((TOK, TOK), F32), IN_VMEM),
         (sds((1, 384), F32), IN_VMEM),
         (sds((D, D), BF16), IN_PLACE),
+        (sds((3, D, D), BF16), IN_PLACE),
         (sds((6, ROWS, 128), F32), IN_VMEM),
         (sds((HEADS, ROWS, 128), BF16), IN_VMEM),
         (sds((5 * ROWS, 2 * COLS), BF16), IN_PLACE),
@@ -664,23 +705,126 @@
             VMEM((1, 40, D), BF16),
             VMEM((1, 40, 640), BF16),
             VMEM((1, 80, 640), BF16),
+            VMEM((3, 40, D), BF16),
+            VMEM((3, 40, 640), BF16),
+            VMEM((3, 80, 640), BF16),
             VMEM((1, D, D), BF16),
             VMEM((5 * ROWS, 2 * COLS), BF16),
             VMEM((HEADS, 64, ROWS), F32),
             VMEM((HEADS, 8, ROWS), F32),
             DMA((10,)),
             DMA((10,)),
-            DMA,
-            DMA,
+            DMA((2,)),
+            DMA((2,)),
             DMA((7,)),
             DMA((5,)),
             DMA((5,)),
         ]
         + ring_scratch()
+        + ring_scratch()
         + tally_scratch((8, 128)),
         compiler_params=params(0),
         name="front",
     )(hidden, teacher, *others)
+
+
+class Spread:
+    def __init__(self, ref, send, recv):
+        z, x, c, y = spot()
+        self.ref, self.send, self.recv, self.y = ref, send, recv, y
+        self.to = {way: device(z, x, c, wrap(y + way)) for way in (1, -1)}
+
+    def full(self, way):
+        rows = pl.ds(pl.multiple_of(TOK * self.y, TOK), TOK)
+        k = 0 if way > 0 else 1
+        return remote(self.ref.at[rows], self.ref.at[rows], self.send.at[k], self.recv.at[k], self.to[way])
+
+    def relay(self, way):
+        half = TOK // 2
+        at = TOK * wrap(self.y - way) + (0 if way > 0 else half)
+        rows = pl.ds(pl.multiple_of(at, half), half)
+        k = 2 if way > 0 else 3
+        return remote(self.ref.at[rows], self.ref.at[rows], self.send.at[k], self.recv.at[k], self.to[way])
+
+    def start(self):
+        self.full(1).start()
+        self.full(-1).start()
+
+    def sides(self):
+        self.full(1).wait_recv()
+        self.relay(1).start()
+        self.full(-1).wait_recv()
+        self.relay(-1).start()
+
+    def opposite(self):
+        self.relay(1).wait_recv()
+        self.relay(-1).wait_recv()
+
+    def close(self):
+        for way in (1, -1):
+            self.full(way).wait_send()
+            self.relay(way).wait_send()
+
+
+HALF = TOK // 2
+OWN, LEFT, RIGHT, OPPOSITE = range(4)
+
+
+def position(slot, h):
+    if slot == OWN:
+        at = HALF * h
+    elif slot == OPPOSITE:
+        at = 6 * HALF + HALF * h
+    else:
+        at = 2 * HALF * (1 + h) + (HALF if slot == RIGHT else 0)
+    return at if isinstance(h, int) else pl.multiple_of(at, HALF)
+
+
+class Halves:
+    def __init__(self, ref, send, recv):
+        z, x, c, y = spot()
+        self.ref, self.send, self.recv = ref, send, recv
+        self.to = {way: device(z, x, c, wrap(y + way)) for way in (1, -1)}
+
+    def full(self, h, way):
+        src = self.ref.at[pl.ds(position(OWN, h), HALF)]
+        dst = self.ref.at[pl.ds(position(LEFT if way > 0 else RIGHT, h), HALF)]
+        k = 0 if way > 0 else 1
+        return remote(src, dst, self.send.at[h, k], self.recv.at[h, k], self.to[way])
+
+    def relay(self, h, way):
+        part = HALF // 2
+        off = 0 if way > 0 else part
+        src = pl.multiple_of(position(LEFT if way > 0 else RIGHT, h) + off, part)
+        dst = pl.multiple_of(position(OPPOSITE, h) + off, part)
+        k = 2 if way > 0 else 3
+        return remote(
+            self.ref.at[pl.ds(src, part)],
+            self.ref.at[pl.ds(dst, part)],
+            self.send.at[h, k],
+            self.recv.at[h, k],
+            self.to[way],
+        )
+
+    def start(self, h):
+        self.full(h, 1).start()
+        self.full(h, -1).start()
+
+    def sides(self, h):
+        self.full(h, 1).wait_recv()
+        self.relay(h, 1).start()
+        self.full(h, -1).wait_recv()
+        self.relay(h, -1).start()
+
+    def opposite(self, h):
+        self.relay(h, 1).wait_recv()
+        self.relay(h, -1).wait_recv()
+
+    def close(self):
+        for h in range(2):
+            for way in (1, -1):
+                self.full(h, way).wait_send()
+                self.relay(h, way).wait_send()
 
 
 def mix_forward(states, branch, alphas):
@@ -717,13 +861,10 @@
     rates,
     up_gain_in,
     gate_gain_in,
-    gate_w,
-    up_w,
-    down_w,
     weights,
+    w_rest,
     output,
-    attn_grad,
-    d_att,
+    attn_low,
     res_zero,
     small,
     gate_out,
@@ -737,9 +878,6 @@
     w_out,
     w_all,
     grads,
-    shard,
-    shard_sib,
-    own_block,
     raw_gate,
     raw_up,
     send_buf,
@@ -749,14 +887,9 @@
     state,
     normed,
     scales,
+    turned,
     w_sem,
     g_sem,
-    s_send,
-    s_recv,
-    b_send,
-    b_recv,
-    b_hsend,
-    b_hrecv,
     ag_send,
     ag_recv,
     rs_send,
@@ -768,119 +901,108 @@
     peers = [device(z, x, c, wrap(y + d)) for d in range(4)]
     load = pltpu.make_async_copy(weights.at[:, pl.ds(0, 384)], w_out, w_sem.at[0])
     load.start()
-    shard[0] = gate_w[...]
-    shard[1] = up_w[...]
-    shard[2] = down_w[...]
+    load_rest = pltpu.make_async_copy(w_rest, w_all, w_sem.at[1])
+    load_rest.start()
     up_gain = up_gain_in[...].reshape(1, D)
     gate_gain = gate_gain_in[...].reshape(1, D)
     w_gate, w_up, w_down = (w_all.at[k] for k in range(3))
-    sibling = device(z, x, 1 - c, y)
-    ring_peers = [device(z, wrap(x + d), c, y) for d in (1, 3)]
-    ring_peers += [device(wrap(z + d), x, c, y) for d in (1, 3)]
-    meet(peers[1:] + ring_peers + [sibling])
-    ours, theirs = lane_halves(c)
-    ring = Ring(
-        own_block, lane_slab(w_all, ours), lane_part(w_all, ours), b_send, b_recv, b_hsend, b_hrecv
-    )
-    head = remote(shard.at[:, :, theirs], shard_sib, s_send, s_recv, sibling)
-    head.start()
-    my_rows = pl.ds(pl.multiple_of(TOK * y, TOK), TOK)
-
-    def rows_of(k):
-        return pl.ds(pl.multiple_of(TOK * wrap(y - k), TOK), TOK)
+    meet(peers[1:])
+    places = {LEFT: 3, RIGHT: 1, OPPOSITE: 2}
+
+    def rows_of(off):
+        return pl.ds(pl.multiple_of(TOK * wrap(y + off), TOK), TOK)
 
     def feats(k):
         return pl.ds(pl.multiple_of(COLS * k, 64), COLS)
 
-    def back_to(k):
-        return device(z, x, c, wrap(y - k))
-
-    def scatter(stage, k):
+    def half_rows(h):
+        return pl.ds(pl.multiple_of(HALF * h, HALF), HALF)
+
+    def scatter(stage, h, slot):
         return remote(
-            send_buf.at[stage, k - 1],
-            got_buf.at[stage, k - 1],
-            rs_send.at[stage, k],
-            rs_recv.at[stage, k],
-            back_to(k),
+            send_buf.at[stage, h, slot - 1],
+            got_buf.at[stage, h, slot - 1],
+            rs_send.at[stage, h, slot],
+            rs_recv.at[stage, h, slot],
+            device(z, x, c, wrap(y + places[slot])),
         )
 
-    def spread(stage, src, k):
-        return remote(
-            src.at[my_rows],
-            src.at[my_rows],
-            ag_send.at[stage, k],
-            ag_recv.at[stage, k],
-            device(z, x, c, wrap(y + k)),
-        )
-
-    def give(stage, k, part):
-        @pl.when(k == 0)
-        def _():
-            own_part[...] = part
-
-        @pl.when(k > 0)
-        def _():
-            send_buf[stage, k - 1] = part.astype(BF16)
-            scatter(stage, k).start()
-
-    def collect(stage):
-        total = own_part[...]
-        for k in (1, 2, 3):
-            scatter(stage, k).wait_recv()
-            total = total + got_buf[stage, k - 1].astype(F32)
+    def give(stage, h, slot, part):
+        send_buf[stage, h, slot - 1] = part.astype(BF16)
+        scatter(stage, h, slot).start()
+
+    def collect(stage, h):
+        total = own_part[half_rows(h), :]
+        for slot in (LEFT, RIGHT, OPPOSITE):
+            scatter(stage, h, slot).wait_recv()
+            total = total + got_buf[stage, h, slot - 1].astype(F32)
         return total
 
-    def announce(stage, ref, value):
-        ref[my_rows, :] = value.astype(BF16)
-        for k in (2, 1, 3):
-            spread(stage, ref, k).start()
-
-    def each(body, stage=None, ref=None):
-        def step(k, carry):
-            if ref is not None:
-
-                @pl.when(k > 0)
+    def both(body):
+        def step(h, carry):
+            body(h)
+            return carry
+
+        lax.fori_loop(0, 2, step, 0)
+
+    def flow(stage, spread, compute):
+        def step(i, carry):
+            @pl.when(i == 1)
+            def _():
+                spread.sides(0)
+
+            part = compute(pl.ds(pl.multiple_of(TOK * i, TOK), TOK))
+
+            @pl.when(i == 0)
+            def _():
+                own_part[...] = part
+
+            @pl.when(i > 0)
+            def _():
+                h = i - 1
+                give(stage, h, LEFT, part[:HALF])
+                give(stage, h, RIGHT, part[HALF:])
+
+                @pl.when(i == 1)
                 def _():
-                    spread(stage, ref, k).wait_recv()
-
-            body(k)
+                    spread.sides(1)
+
+                spread.opposite(h)
+                give(stage, h, OPPOSITE, compute(pl.ds(position(OPPOSITE, h), HALF)))
+
             return carry
 
-        lax.fori_loop(0, 4, step, 0)
+        lax.fori_loop(0, 3, step, 0)
+
+    ones = Halves(in_one, ag_send.at[0], ag_recv.at[0])
+    backs = Halves(mlp_grad, ag_send.at[1], ag_recv.at[1])
 
     load.wait()
-    for k in (2, 1, 3):
-        send_buf[0, k - 1] = dot_nt(att[rows_of(k), :], w_out[...]).astype(BF16)
-        scatter(0, k).start()
-    head.wait()
-    join_cores(c, shard, shard_sib, own_block, ours)
-    ring.open()
-    ring_own = pltpu.make_async_copy(own_block, ring.slab(ring.block(0, 0)), w_sem.at[1])
-    ring_own.start()
-    own_part[...] = dot_nt(att[my_rows, :], w_out[...])
-    ring.near()
-    ring.turn(0)
-    ring.far()
-    attn = collect(0)
-    states = hid_tok[...].astype(F32)
-    one, normed_one, branch_one, scale_one = mix_forward(states, attn, rates[0:1, :])
-    announce(0, in_one, one)
-    state[0] = one
-    normed[0] = normed_one
-    scales[0] = jnp.broadcast_to(branch_one, (TOK, 128))
-    scales[1] = jnp.broadcast_to(scale_one, (TOK, 128))
-    ring.turn(3)
-    ring.turn(1)
-    ring.end(0)
-    ring.turn(2)
-    ring.end(3)
-    ring.end(1)
-    ring.end(2)
-    ring_own.wait()
-    ring.arrive()
-
-    def feed(k):
-        rows = rows_of(k)
+    for slot in (OPPOSITE, LEFT, RIGHT):
+        part = dot_nt(att[rows_of(places[slot]), :], w_out[...])
+        give(0, 0, slot, part[:HALF])
+        send_buf[0, 1, slot - 1] = part[HALF:].astype(BF16)
+    for slot in (OPPOSITE, LEFT, RIGHT):
+        scatter(0, 1, slot).start()
+    own_part[...] = dot_nt(att[rows_of(0), :], w_out[...])
+    small[...] = jnp.zeros_like(small)
+
+    def first_mix(h):
+        rows = half_rows(h)
+        attn = collect(0, h)
+        states = hid_tok[rows, :].astype(F32)
+        one, normed_one, branch_one, scale_one = mix_forward(states, attn, rates[0:1, :])
+        in_one[rows, :] = one.astype(BF16)
+        ones.start(h)
+        state[0, rows, :] = one
+        normed[rows, :] = normed_one
+        scales[0, rows, :] = jnp.broadcast_to(branch_one, (HALF, 128))
+        scales[1, rows, :] = jnp.broadcast_to(scale_one, (HALF, 128))
+
+    both(first_mix)
+    load_rest.wait()
+
+    def feed(rows):
         block = in_one[rows, :]
         gate_raw = dot_nn(block, w_gate[...])
         raw_gate[rows, :] = gate_raw
@@ -889,43 +1011,48 @@
         g, q = swiglu_parts(gate_raw, up_raw, gate_gain, up_gain)
         low = (up_gain * up_raw * (g * q)).astype(BF16)
         product[rows, :] = low
-        give(1, k, dot_nt(low, w_down[...]))
-
-    each(feed, 0, in_one)
-    mlp = collect(1)
-    one = state[0]
-    two, normed_two, branch_two, scale_two = mix_forward(one, mlp, rates[1:2, :])
+        return dot_nt(low, w_down[...])
+
+    flow(1, ones, feed)
+    factor = 16384 * math.sqrt(D) / count[0:1, 0:1]
+
+    def second_mix(h):
+        rows = half_rows(h)
+        mlp = collect(1, h)
+        one = state[0, rows, :]
+        two, normed_two, branch_two, scale_two = mix_forward(one, mlp, rates[1:2, :])
+        errors = two - tea[rows, :].astype(F32)
+        weight = mask[rows, 0:1]
+        seed = factor * (weight * errors)
+        res_one, mlp_back, rate_two = mix_backward(
+            seed, one, normed_two, branch_two, two, scale_two, rates[1:2, :]
+        )
+        mlp_grad[rows, :] = mlp_back.astype(BF16)
+        backs.start(h)
+        state[1, rows, :] = res_one
+        turned[rows, :] = two
+        small[1:2, :] += rate_two
+        loss = jnp.sum(jnp.sum(weight * errors * errors, axis=1, keepdims=True), axis=0, keepdims=True)
+        small[4:5, :] += jnp.broadcast_to(loss, (1, D))
+
+    both(second_mix)
     for g in range(10):
-        out_buf[128 * g : 128 * g + 128, :] = two[:, 128 * g : 128 * g + 128].T.astype(BF16)
+        lanes = slice(128 * g, 128 * g + 128)
+        out_buf[lanes, :] = turned[:, lanes].T.astype(BF16)
     out_copies = []
     for k in (1, 2, 3):
         copy = remote(
             out_buf.at[feats(wrap(y + k))],
-            output.at[:, my_rows],
+            output.at[:, rows_of(0)],
             o_send.at[k],
             o_recv.at[k],
             device(z, x, c, wrap(y + k)),
         )
+        copy.start()
         out_copies.append(copy)
-    errors = two - tea[...].astype(F32)
-    weight = mask[:, 0:1]
-    loss = jnp.sum(weight * errors * errors)
-    factor = 16384 * math.sqrt(D) / count[0:1, 0:1]
-    seed = factor * (weight * errors)
-    res_one, mlp_back, rate_two = mix_backward(
-        seed, one, normed_two, branch_two, two, scale_two, rates[1:2, :]
-    )
-    announce(1, mlp_grad, mlp_back)
-    for copy in out_copies:
-        copy.start()
-    output[:, my_rows] = out_buf[feats(y), :]
-    small[...] = jnp.zeros_like(small)
-    small[1:2, :] = rate_two
-    small[4:5, :] = jnp.broadcast_to(loss, (1, D))
-    state[1] = res_one
-
-    def unfeed(k):
-        rows = rows_of(k)
+    output[:, rows_of(0)] = out_buf[feats(y), :]
+
+    def unfeed(rows):
         grad = dot_nn(mlp_grad[rows, :], w_down[...])
         gate_raw = raw_gate[rows, :]
         up_raw = raw_up[rows, :]
@@ -939,9 +1066,9 @@
         gate_back = (slope * gate_gain).astype(BF16)
         up_low[rows, :] = up_back
         gate_low[rows, :] = gate_back
-        give(2, k, dot_nt(gate_back, w_gate[...]) + dot_nt(up_back, w_up[...]))
-
-    each(unfeed, 1, mlp_grad)
+        return dot_nt(gate_back, w_gate[...]) + dot_nt(up_back, w_up[...])
+
+    flow(2, backs, unfeed)
 
     def weight_grad(j, left, right, out):
         def step(k, carry):
@@ -953,43 +1080,42 @@
         pltpu.make_async_copy(grads.at[j], out, g_sem.at[j]).start()
 
     weight_grad(2, mlp_grad, product, down_out)
-    grad_one = state[1] + collect(2)
-    states = hid_tok[...].astype(F32)
-    res, attn_back, rate_one = mix_backward(
-        grad_one,
-        states,
-        normed[0],
-        scales[0, :, 0:1],
-        state[0],
-        scales[1, :, 0:1],
-        rates[0:1, :],
-    )
-    announce(2, attn_grad, attn_back)
-    small[0:1, :] = rate_one
-    for g in range(10):
-        res_zero[128 * g : 128 * g + 128, :] = res[:, 128 * g : 128 * g + 128].T
-
-    def unproject(k):
-        rows = rows_of(k)
-        d_att[rows, :] = dot_nn(attn_grad[rows, :], w_out[...]).astype(BF16)
-
     weight_grad(0, in_one, gate_low, gate_out)
     weight_grad(1, in_one, up_low, up_out)
-    each(unproject, 2, attn_grad)
+
+    def third_mix(h):
+        rows = half_rows(h)
+        grad_one = state[1, rows, :] + collect(2, h)
+        res, attn_back, rate_one = mix_backward(
+            grad_one,
+            hid_tok[rows, :].astype(F32),
+            normed[rows, :],
+            scales[0, rows, 0:1],
+            state[0, rows, :],
+            scales[1, rows, 0:1],
+            rates[0:1, :],
+        )
+        attn_low[rows, :] = attn_back.astype(BF16)
+        small[0:1, :] += rate_one
+        turned[rows, :] = res
+
+    both(third_mix)
+    for g in range(10):
+        lanes = slice(128 * g, 128 * g + 128)
+        res_zero[lanes, :] = turned[:, lanes].T
     for j, out in enumerate((gate_out, up_out, down_out)):
         pltpu.make_async_copy(grads.at[j], out, g_sem.at[j]).wait()
-    ring.close()
-    for k in (1, 2, 3):
+    for slot in (LEFT, RIGHT, OPPOSITE):
         for stage in range(3):
-            scatter(stage, k).wait_send()
-        spread(0, in_one, k).wait_send()
-        spread(1, mlp_grad, k).wait_send()
-        spread(2, attn_grad, k).wait_send()
+            for h in range(2):
+                scatter(stage, h, slot).wait_send()
+    ones.close()
+    backs.close()
     for copy in out_copies:
         copy.wait()
 
 
-def middle(vmem_args, weights):
+def middle(vmem_args, placed_args):
     sds = jax.ShapeDtypeStruct
     wide = VMEM((ROWS, D), BF16)
     square = sds((D, D), BF16)
@@ -997,16 +1123,15 @@
         middle_kernel,
         out_shape=(
             sds((COLS, ROWS), BF16),
-            sds((ROWS, D), BF16),
-            sds((ROWS, 384), BF16),
+            sds((TOK, D), BF16),
             sds((D, TOK), F32),
             sds((8, D), F32),
             square,
             square,
             square,
         ),
-        in_specs=[IN_VMEM] * len(vmem_args) + [IN_PLACE],
-        out_specs=(IN_VMEM,) * 5 + (IN_PLACE,) * 3,
+        in_specs=[IN_VMEM] * len(vmem_args) + [IN_PLACE] * len(placed_args),
+        out_specs=(IN_VMEM,) * 4 + (IN_PLACE,) * 3,
         scratch_shapes=[
             wide,
             wide,
@@ -1016,35 +1141,28 @@
             VMEM((D, 384), BF16),
             VMEM((3, D, D), BF16),
             VMEM((3, D, D), BF16),
-            VMEM((3, 40, D), BF16),
-            VMEM((3, 40, 640), BF16),
-            VMEM((3, 80, 640), BF16),
             VMEM((ROWS, D), F32),
             VMEM((ROWS, D), F32),
-            VMEM((3, 3, TOK, D), BF16),
-            VMEM((3, 3, TOK, D), BF16),
+            VMEM((3, 2, 3, HALF, D), BF16),
+            VMEM((3, 2, 3, HALF, D), BF16),
             VMEM((TOK, D), F32),
             VMEM((D, TOK), BF16),
             VMEM((2, TOK, D), F32),
-            VMEM((1, TOK, D), F32),
+            VMEM((TOK, D), F32),
             VMEM((2, TOK, 128), F32),
+            VMEM((TOK, D), F32),
             DMA((2,)),
             DMA((3,)),
-            DMA,
-            DMA,
-        ]
-        + ring_scratch()
-        + [
-            DMA((3, 4)),
-            DMA((3, 4)),
-            DMA((3, 4)),
-            DMA((3, 4)),
+            DMA((2, 2, 4)),
+            DMA((2, 2, 4)),
+            DMA((3, 2, 4)),
+            DMA((3, 2, 4)),
             DMA((4,)),
             DMA((4,)),
         ],
         compiler_params=params(1),
         name="middle",
-    )(*vmem_args, weights)
+    )(*vmem_args, *placed_args)
 
 
 class Fold:
@@ -1052,15 +1170,10 @@
         z, x, c, y = spot()
         self.z, self.x, self.c = z, x, c
         self.z_heavy = z_heavy
-        if z_heavy:
-            self.first = lambda d: device(z, wrap(x + d), c, y)
-            self.second = lambda d: device(wrap(z + d), x, c, y)
-            self.at_first = x
-        else:
-            self.first, self.second, _ = torus(z, x, c, y)
-            self.at_first = x * (1 - c) + z * c
+        self.first, self.second, _ = torus(z, x, c, y, z_heavy)
+        self.at_first = x if z_heavy else x * (1 - c) + z * c
         self.sibling = device(z, x, 1 - c, y)
-        self.own, self.sib, self.got_two, self.mid, self.got_one, self.fin = bufs
+        self.own, self.sib, self.relays, self.got_two, self.mid, self.got_one, self.fin = bufs
         self.l_sem, self.h_send, self.h_recv, self.b_send, self.b_recv, self.a_send, self.a_recv, self.f_send, self.f_recv = sems
         self.count = self.own.shape[0]
         self.lanes = pl.ds(pl.multiple_of(640 * c, 128), 640)
@@ -1095,10 +1208,14 @@
                     self.handed(j, d, src.at[wrap(z + d), :, :, self.other]).start()
                     self.fetched(j, d, src.at[:, wrap(x + d), :, self.lanes]).start()
 
-    def pair(self, d):
-        return remote(
-            self.own.at[:, d], self.got_two.at[:, d - 1], self.b_send.at[d], self.b_recv.at[d], self.second(d)
-        )
+    def pair(self, k):
+        way = 1 if k % 2 == 0 else -1
+        at = pl.ds(0 if k in (0, 3, 4) else 2, 2)
+        if k < 2:
+            src, dst = self.own.at[:, 2, at], self.relays.at[:, k]
+        else:
+            src, dst = self.own.at[:, 1 if way > 0 else 3, at], self.got_two.at[:, k % 2, at]
+        return remote(src, dst, self.b_send.at[k], self.b_recv.at[k], self.second(way))
 
     def last(self, e):
         return remote(
@@ -1118,18 +1235,31 @@
             return carry
 
         lax.fori_loop(0, 4 * self.count, each, 0)
-        if d:
-            self.pair(d).start()
+        for k in {2: (0, 1), 1: (2,), 3: (3,), 0: ()}[d]:
+            self.pair(k).start()
+
+    def relay(self):
+        for k, d, off in ((0, 1, 0), (1, 3, 2)):
+            self.pair(k).wait_recv()
+
+            def each(i, carry, k=k, d=d, off=off):
+                j, a = lax.div(i, 2), lax.rem(i, 2)
+                total = self.own[j, d, off + a].astype(F32) + self.relays[j, k, a].astype(F32)
+                self.own[j, d, off + a] = total.astype(BF16)
+                return carry
+
+            lax.fori_loop(0, 2 * self.count, each, 0)
+            self.pair(4 + k).start()
 
     def whole(self, j, at):
         total = self.own[j, 0, at].astype(F32)
-        for d in (1, 2, 3):
-            total = total + self.got_two[j, d - 1, at].astype(F32)
+        for k in range(2):
+            total = total + self.got_two[j, k, at].astype(F32)
         return total
 
     def cross(self):
-        for d in (1, 2, 3):
-            self.pair(d).wait_recv()
+        for k in range(2, 6):
+            self.pair(k).wait_recv()
         for e in (2, 1, 3):
 
             def each(j, carry, e=e):
@@ -1162,9 +1292,10 @@
 
     def close(self, out):
         self.give(out).wait()
-        for d in (1, 2, 3):
-            self.pair(d).wait_send()
-            self.last(d).wait_send()
+        for k in range(6):
+            self.pair(k).wait_send()
+        for e in (1, 2, 3):
+            self.last(e).wait_send()
         for j in range(self.count):
             for d in range(4):
                 self.handed(j, d, self.sib.at[j, d]).wait_send()
@@ -1175,15 +1306,16 @@
     return [
         VMEM((count, 4, 4) + block, BF16),
         VMEM((count, 4, 4) + block, BF16),
-        VMEM((count, 3, 4) + block, BF16),
+        VMEM((count, 2, 2) + block, BF16),
+        VMEM((count, 2, 4) + block, BF16),
         VMEM((count, 3) + block, BF16),
         VMEM((count, 3) + block, BF16),
         VMEM((count,) + block, F32),
         DMA((count, 4)),
         DMA((count, 4)),
         DMA((count, 4)),
-        DMA((4,)),
-        DMA((4,)),
+        DMA((6,)),
+        DMA((6,)),
         DMA((4,)),
         DMA((4,)),
         DMA,
@@ -1204,7 +1336,7 @@
     q_pad,
     out_t,
     lse,
-    d_att,
+    attn_low,
     att,
     gains,
     cos_block,
@@ -1217,7 +1349,6 @@
     raw_in,
     hid_in,
     w_in,
-    attn_in,
     m0,
     m1,
     m2,
@@ -1235,6 +1366,7 @@
     hid_t,
     w_first,
     attn,
+    d_att,
     d_pad,
     delta,
     q_acc,
@@ -1264,10 +1396,12 @@
     y_recv,
     v_send,
     v_recv,
+    g_send,
+    g_recv,
     *rest,
 ):
-    m_bufs, m_sems, rest = rest[:6], rest[6:15], rest[15:]
-    f_bufs, f_sems, rest = rest[:6], rest[6:15], rest[15:]
+    m_bufs, m_sems, rest = rest[:7], rest[7:16], rest[16:]
+    f_bufs, f_sems, rest = rest[:7], rest[7:16], rest[16:]
     t_accs, t_parts, t_send, t_recv = rest
     z, x, c, y = spot()
     place = 2 * x + c
@@ -1286,13 +1420,19 @@
     loads = [
         pltpu.make_async_copy(src, dst, in_sem.at[5 + k])
         for k, (src, dst) in enumerate(
-            ((raw_in, raw), (attn_in, attn), (w_in, w_first), (hid_in, hid_t))
+            ((w_in, w_first), (raw_in, raw), (hid_in, hid_t))
         )
     ]
     meet(across + tally.peers[0] + tally.peers[1] + tally.peers[2])
     fold_m = Fold(m_bufs, m_sems, True)
     fold_f = Fold(f_bufs, f_sems, False)
+    my_rows = pl.ds(pl.multiple_of(TOK * y, TOK), TOK)
+    attn[my_rows, :] = attn_low[...]
+    spread = Spread(attn, g_send, g_recv)
+    spread.start()
     fold_m.open([m0, m1, m2])
+    for load in loads:
+        load.start()
     side_src[...] = jnp.zeros_like(side_src)
     for k in range(4):
         lanes = slice(COLS * k, COLS * (k + 1))
@@ -1304,8 +1444,21 @@
 
     for k in (1, 2, 3):
         side(k).start()
-    for load in loads:
-        load.start()
+    loads[0].wait()
+
+    def unproject(k):
+        rows = pl.ds(pl.multiple_of(TOK * wrap(y + k), TOK), TOK)
+        d_att[rows, :] = dot_nn(attn[rows, :], w_first[:, 0:384]).astype(BF16)
+
+    unproject(0)
+    fold_m.add(2)
+    spread.sides()
+    fold_m.add(1)
+    unproject(1)
+    unproject(3)
+    fold_m.add(3)
+    spread.opposite()
+    unproject(2)
 
     for h in range(HEADS):
         d_pad[h] = pad_head(d_att, (h + 1) // 2, (h + 1) % 2)
@@ -1394,7 +1547,7 @@
 
     for load in win_loads:
         load.wait()
-    folds = {2: 2, 3: 1, 5: 3, 7: 0}
+    folds = {3: 0}
 
     def step(i, carry):
         k = lax.div(i, 2)
@@ -1416,10 +1569,14 @@
             def _(d=d):
                 fold_m.add(d)
 
+        @pl.when(i == 5)
+        def _():
+            fold_m.relay()
+
         return carry
 
     lax.fori_loop(0, 10, step, 0)
-    for load in loads:
+    for load in loads[1:]:
         load.wait()
     cosine, sine = rope_wide(cos_block, sin_block, turn)
     pack[:, 128:384] = jnp.zeros((ROWS, 256), BF16)
@@ -1504,6 +1661,7 @@
     project(y)
     for d in (2, 1, 3, 0):
         fold_f.add(d)
+    fold_f.relay()
     for k in (1, 2, 3):
         grad_copy(k).wait_recv()
         hidden_grad[...] += y_got_buf[k - 1].astype(F32)
@@ -1528,6 +1686,7 @@
     for k in (1, 2, 3):
         grad_copy(k).wait_send()
         side(k).wait_send()
+    spread.close()
 
     @pl.when(x > 0)
     def _():
@@ -1564,6 +1723,7 @@
             VMEM((D, ROWS), BF16),
             VMEM((D, D), BF16),
             VMEM((ROWS, D), BF16),
+            VMEM((ROWS, 384), BF16),
             VMEM((HEADS, ROWS, 128), BF16),
             VMEM((HEADS, 8, ROWS), F32),
             VMEM((HEADS, 64, ROWS), F32),
@@ -1589,6 +1749,8 @@
             DMA((4,)),
             DMA((4,)),
             DMA((4,)),
+            DMA((4,)),
+            DMA((4,)),
         ]
         + fold_scratch(3)
         + fold_scratch(1)
@@ -1644,6 +1806,7 @@
 ):
     ropes = rope_constants()
     others = (query_weight, key_weight, value_weight, out_weight.T)
+    others += (gate_weight, up_weight, down_weight.T)
     others += (attention_rate, feedforward_rate, valid_mask, segments, score_gain, *ropes)
     (
         hid_t,
@@ -1654,6 +1817,7 @@
         mask,
         gains,
         weights,
+        w_rest,
         raw,
         q_pad,
         win,
@@ -1662,7 +1826,7 @@
         lse,
         starts,
     ) = front(hidden.T, teacher.T, others)
-    output, attn_grad, d_att, res_t, small, *grads = middle(
+    output, attn_low, res_t, small, *grads = middle(
         (
             att,
             hid_tok,
@@ -1672,15 +1836,12 @@
             rates,
             up_gain,
             gate_gain,
-            gate_weight,
-            up_weight,
-            down_weight.T,
         ),
-        weights,
+        (weights, w_rest),
     )
     results = tail(
-        (starts, q_pad, out_t, lse, d_att, att, gains, *ropes, res_t, small, count),
-        (win, raw, hid_t, weights, attn_grad) + tuple(g.reshape(4, 4, 80, D) for g in grads),
+        (starts, q_pad, out_t, lse, attn_low, att, gains, *ropes, res_t, small, count),
+        (win, raw, hid_t, weights) + tuple(g.reshape(4, 4, 80, D) for g in grads),
     )
     results = emit(results[8], (output,) + tuple(results[:8]))
     output, hidden_grad, query_g, key_g, value_g, out_g, gate_g, up_g, down_g = results[:9]

time: 293 us -> 253 us (0.86)
  Pallas kernels: 292 us -> 252 us
    pallas_call x1, Pallas kernels: 125 us -> 76 us  [middle(): pl.pallas_call(middle_kernel, out_shape=(sds((COLS, ROWS), BF16), sds((TO...]
    pallas_call x1, Pallas kernels: 61.6 us -> 75.2 us  [front(): pl.pallas_call(front_kernel, out_shape=tuple((o[0] for o in outs)), in_sp...]
    pallas_call x1, Pallas kernels: 103 us -> 97.7 us  [tail(): pl.pallas_call(tail_kernel, out_shape=tuple((sds(s, F32) for s in shapes)...]
where the time goes in v2:
time: 253 us
  Pallas kernels  252 us (100%)
    pallas_call x1, Pallas kernels, tail(): pl.pallas_call(tail_kernel, out_shape=tuple((sds(s, F32) for s in shapes)...  97.7 us
    pallas_call x1, Pallas kernels, middle(): pl.pallas_call(middle_kernel, out_shape=(sds((COLS, ROWS), BF16), sds((TO...  76 us
    pallas_call x1, Pallas kernels, front(): pl.pallas_call(front_kernel, out_shape=tuple((o[0] for o in outs)), in_sp...  75.2 us

profile of v2, /device:TPU:1, one launch (start us, length us, event | category | flops | bytes accessed | tf_op | source)
XLA Modules:
  0.0 252.6 jit_solution(16922109073059141012)
XLA Ops:
  0.7 75.2 %front.1 = (bf16[1280,512]{1,0:T(8,128)(2,1)}, bf16[128,1280]{1,0:T(8,128)(2,1)}, bf16[128,1280]{1,0:T(8,128)(2,1)}, f32[2,1280]{1,0:T(2,128)}, f32[8,128]{1,0:T...) custom-call(bf16[320,512]{1,0:T(8,128)(2,1)} %bitcast.15, ...), custom_call_target="tpu_custom_call" | custom-call | tf_op jit(solution)/shard_map/front/pallas_call | solution.py:692
  75.9 76.0 %middle.1 = (bf16[320,512]{1,0:T(8,128)(2,1)}, bf16[128,1280]{1,0:T(8,128)(2,1)}, f32[1280,128]{1,0:T(8,128)}, f32[8,1280]{1,0:T(8,128)}, bf16[1280,1280]{1,0:T(...) custom-call(bf16[512,384]{1,0:T(8,128)(2,1)} %get-tuple-element.66.att, ...), custom_call_target="tpu_custom_call" | custom-call | tf_op jit(solution)/shard_map/middle/pallas_call | solution.py:1122
  151.9 97.7 %tail.1 = (f32[320,512]{1,0:T(8,128)}, f32[40,320]{1,0:T(8,128)}, f32[40,320]{1,0:T(8,128)}, f32[40,320]{1,0:T(8,128)}, f32[40,320]{1,0:T(8,128)}, /*index=5*/f3...) custom-call(s32[1,512]{1,0:T(1,128)} %get-tuple-element.62.starts, ...), custom_call_target="tpu_custom_call" | custom-call | tf_op jit(solution)/shard_map/tail/pallas_call | solution.py:1715
  249.6 2.8 %emit.1 = (bf16[320,512]{1,0:T(8,128)(2,1)}, f32[320,512]{1,0:T(8,128)}, f32[40,320]{1,0:T(8,128)}, f32[40,320]{1,0:T(8,128)}, f32[40,320]{1,0:T(8,128)}, /*inde...) custom-call(f32[8,1280]{1,0:T(8,128)} %get-tuple-element.84.sums, ...), custom_call_target="tpu_custom_call" | custom-call | tf_op jit(solution)/shard_map/emit/pallas_call | solution.py:1779

commit v3 on v2

--- a/solution.py
+++ b/solution.py
@@ -16,6 +16,7 @@
 TOK = 128
 COLS = 320
 TILE = 256
+UP = 176
 F32 = jnp.float32
 BF16 = jnp.bfloat16
 MESH = pl.DeviceIdType.MESH
@@ -373,6 +374,7 @@
     own_b,
     w_first,
     win,
+    transit,
     o_acc,
     l_acc,
     y_send,
@@ -390,6 +392,10 @@
     b_recv,
     b_hsend,
     b_hrecv,
+    c_send,
+    c_recv,
+    c_hsend,
+    c_hrecv,
     t_accs,
     t_parts,
     t_send,
@@ -415,8 +421,25 @@
 
     ours, theirs = lane_halves(c)
     ring_a = Ring(own_block, lane_slab(w_first, ours), lane_part(w_first, ours), a_send, a_recv, a_hsend, a_hrecv)
+    w_pair, w_last = w_rest.at[pl.ds(0, 2)], w_rest.at[pl.ds(2, 1)]
     ring_b = Ring(
-        own_b, lane_slab(w_rest, ours), lane_part(w_rest, ours), b_send, b_recv, b_hsend, b_hrecv, True
+        own_b.at[pl.ds(0, 2)],
+        lane_slab(w_pair, ours),
+        lane_part(w_pair, ours),
+        b_send,
+        b_recv,
+        b_hsend,
+        b_hrecv,
+        True,
+    )
+    ring_c = Ring(
+        own_b.at[pl.ds(2, 1)],
+        lane_slab(w_last, ours),
+        lane_part(w_last, ours),
+        c_send,
+        c_recv,
+        c_hsend,
+        c_hrecv,
     )
     head = remote(shard.at[:, :, theirs], shard_sib, s_send.at[0], s_recv.at[0], sibling)
     head.start()
@@ -468,11 +491,12 @@
     ring_a.near()
     head_b.wait()
     join_cores(c, shard_b, shard_b_sib, own_b, ours)
-    own_rest = pltpu.make_async_copy(own_b, ring_b.slab(ring_b.block(0, 0)), local_sem.at[3])
+    own_rest = pltpu.make_async_copy(own_b, lane_slab(w_rest, ours)(ring_b.block(0, 0)), local_sem.at[3])
     own_rest.start()
     ring_a.turn(0)
     ring_a.far()
     ring_b.open()
+    ring_c.open()
     hid_r.wait_recv()
     hid_f_ref = hid_t.at[pl.ds(pl.multiple_of(COLS * wrap(y - 1), 64), 160)]
     hid_f = remote(hid_f_ref, hid_f_ref, y_send.at[2], y_recv.at[2], across[0])
@@ -502,6 +526,7 @@
     own_a.wait()
     ring_a.arrive()
     ring_b.near()
+    ring_c.near()
     w_save = pltpu.make_async_copy(w_first.at[0], weights, local_sem.at[5])
     w_save.start()
 
@@ -521,7 +546,27 @@
         return win.at[pl.ds(pl.multiple_of(ROWS * s, ROWS), ROWS)]
 
     one = remote(slot(4), slot(2), k_send.at[0], k_recv.at[0], device(z, wrap(x + 1), c, y))
-    two = remote(slot(4), slot(0), k_send.at[1], k_recv.at[1], device(z, wrap(x + 2), c, y))
+    up = remote(
+        win.at[pl.ds(2 * ROWS, UP)],
+        win.at[pl.ds(0, UP)],
+        k_send.at[1],
+        k_recv.at[1],
+        device(z, wrap(x + 1), c, y),
+    )
+    down = remote(
+        win.at[pl.ds(4 * ROWS + UP, ROWS - UP)],
+        transit,
+        k_send.at[5],
+        k_recv.at[5],
+        device(z, wrap(x - 1), c, y),
+    )
+    down_on = remote(
+        transit,
+        win.at[pl.ds(UP, ROWS - UP)],
+        k_send.at[6],
+        k_recv.at[6],
+        device(z, wrap(x - 1), c, y),
+    )
     own = remote(slot(4), slot(3), k_send.at[2], k_recv.at[2], sibling)
     one_on = remote(slot(2), slot(1 + 2 * c), k_send.at[3], k_recv.at[3], sibling)
     two_on = remote(slot(0), slot(1), k_send.at[4], k_recv.at[4], sibling)
@@ -532,7 +577,7 @@
 
     @pl.when(x < 2)
     def _():
-        two.start()
+        down.start()
 
     @pl.when(c == 0)
     def _():
@@ -550,7 +595,9 @@
 
     ring_b.turn(0)
     ring_b.far()
-    events = ring_b.steps()[3:]
+    ring_c.turn(0)
+    ring_c.far()
+    events = list(zip(ring_b.steps()[3:], ring_c.steps()[3:]))
 
     def tile(t):
         rows = pl.ds(pl.multiple_of(t * TILE, TILE), TILE)
@@ -582,13 +629,23 @@
             one.wait_recv()
             one_on.start()
 
+            @pl.when(x < 3)
+            def _():
+                up.start()
+
+        @pl.when((i == 3) & ((x == 0) | (x == 3)))
+        def _():
+            down.wait_recv()
+            down_on.start()
+
         @pl.when((x > 0) & (((i == 6) & (c == 1)) | ((i == 4) & (c == 0))))
         def _():
             one_on.wait_recv()
 
         @pl.when((x > 1) & (((i == 8) & (c == 1)) | ((i == 6) & (c == 0))))
         def _():
-            two.wait_recv()
+            up.wait_recv()
+            down_on.wait_recv()
 
             @pl.when(c == 1)
             def _():
@@ -602,7 +659,8 @@
 
             @pl.when(i == n + 2)
             def _(event=event):
-                event()
+                event[0]()
+                event[1]()
 
         @pl.when(place + s >= 4)
         def _():
@@ -628,9 +686,11 @@
     wide = jnp.concatenate([jnp.zeros((64, ROWS), F32), out_t[...]], axis=0)
     att[...] = wide.T.astype(BF16)
     ring_b.arrive()
+    ring_c.arrive()
     own_rest.wait()
     ring_a.close()
     ring_b.close()
+    ring_c.close()
     hid_save.wait()
     w_save.wait()
     win_save.wait()
@@ -643,7 +703,15 @@
 
     @pl.when(x < 2)
     def _():
-        two.wait_send()
+        down.wait_send()
+
+    @pl.when((x == 0) | (x == 3))
+    def _():
+        down_on.wait_send()
+
+    @pl.when((x == 1) | (x == 2))
+    def _():
+        up.wait_send()
 
     @pl.when(c == 0)
     def _():
@@ -710,6 +778,7 @@
             VMEM((3, 80, 640), BF16),
             VMEM((1, D, D), BF16),
             VMEM((5 * ROWS, 2 * COLS), BF16),
+            VMEM((ROWS - UP, 2 * COLS), BF16),
             VMEM((HEADS, 64, ROWS), F32),
             VMEM((HEADS, 8, ROWS), F32),
             DMA((10,)),
@@ -717,9 +786,10 @@
             DMA((2,)),
             DMA((2,)),
             DMA((7,)),
-            DMA((5,)),
-            DMA((5,)),
+            DMA((7,)),
+            DMA((7,)),
         ]
+        + ring_scratch()
         + ring_scratch()
         + ring_scratch()
         + tally_scratch((8, 128)),
@@ -1373,11 +1443,12 @@
     d_win,
     sib_one,
     sib_two,
-    sib_own,
     one_buf,
     two_buf,
     got_one,
     got_two,
+    got_part,
+    transit,
     kv_sum,
     pack,
     out_part,
@@ -1471,9 +1542,19 @@
 
     hand_one = remote(slot(d_win, 3 - 2 * c), sib_one, k_send.at[0], k_recv.at[0], sibling)
     hand_two = remote(slot(d_win, 1), sib_two, k_send.at[1], k_recv.at[1], sibling)
-    hand_own = remote(slot(d_win, 3), sib_own, k_send.at[2], k_recv.at[2], sibling)
+    hand_own = remote(slot(d_win, 3), sib_two, k_send.at[2], k_recv.at[2], sibling)
     one = remote(one_buf, got_one, k_send.at[3], k_recv.at[3], device(z, wrap(x + 3), c, y))
-    two = remote(two_buf, got_two, k_send.at[4], k_recv.at[4], device(z, wrap(x + 2), c, y))
+    part_a = remote(
+        two_buf.at[pl.ds(0, UP)], got_part, k_send.at[4], k_recv.at[4], device(z, wrap(x - 1), c, y)
+    )
+    part_b = remote(
+        two_buf.at[pl.ds(UP, ROWS - UP)],
+        transit,
+        k_send.at[5],
+        k_recv.at[5],
+        device(z, wrap(x + 1), c, y),
+    )
+    part_on = remote(transit, got_two, k_send.at[6], k_recv.at[6], device(z, wrap(x + 1), c, y))
 
     def tile(t):
         rows = pl.ds(pl.multiple_of(t * TILE, TILE), TILE)
@@ -1505,7 +1586,8 @@
             @pl.when((c == 0) & (x > 1))
             def _():
                 two_buf[...] = d_win[0:ROWS, :]
-                two.start()
+                part_b.start()
+                part_a.start()
 
         if k == 1:
 
@@ -1529,7 +1611,8 @@
                 two_buf[...] = (
                     d_win[0:ROWS, :].astype(F32) + sib_two[...].astype(F32)
                 ).astype(BF16)
-                two.start()
+                part_b.start()
+                part_a.start()
 
         if k == 3:
 
@@ -1539,6 +1622,14 @@
                 one_buf[...] = (
                     d_win[2 * ROWS : 3 * ROWS, :].astype(F32) + sib_one[...].astype(F32)
                 ).astype(BF16)
+
+                @pl.when(x < 3)
+                def _():
+                    part_a.wait_recv()
+                    one_buf[0:UP, :] = (
+                        one_buf[0:UP, :].astype(F32) + got_part[...].astype(F32)
+                    ).astype(BF16)
+
                 one.start()
 
             @pl.when(c == 1)
@@ -1568,6 +1659,11 @@
             @pl.when(i == n)
             def _(d=d):
                 fold_m.add(d)
+
+        @pl.when((i == 6) & ((x == 0) | (x == 3)))
+        def _():
+            part_b.wait_recv()
+            part_on.start()
 
         @pl.when(i == 5)
         def _():
@@ -1591,12 +1687,13 @@
         gain_parts.append(gain_part)
     out_part[...] = dot_tn(attn[...], att[...])
 
+    fold_m.cross()
     kv_sum[...] = d_win[4 * ROWS :, :].astype(F32)
 
     @pl.when(c == 0)
     def _():
         hand_own.wait_recv()
-        kv_sum[...] += sib_own[...].astype(F32)
+        kv_sum[...] += sib_two[...].astype(F32)
 
     @pl.when(x < 3)
     def _():
@@ -1605,8 +1702,8 @@
 
     @pl.when(x < 2)
     def _():
-        two.wait_recv()
-        kv_sum[...] += got_two[...].astype(F32)
+        part_on.wait_recv()
+        kv_sum[UP:, :] += got_two[...].astype(F32)
 
     for g in range(3):
         grad = kv_sum[:, 128 * g : 128 * g + 128]
@@ -1629,11 +1726,6 @@
     def grad_copy(k):
         return remote(y_send_buf.at[k - 1], y_got_buf.at[k - 1], y_send.at[k], y_recv.at[k], across[k - 1])
 
-    for k in (2, 1, 3):
-        project(wrap(y + k))
-        y_send_buf[k - 1] = hidden_grad[...].astype(BF16)
-        grad_copy(k).start()
-
     extra = side_src[y]
     for k in (1, 2, 3):
         side(k).wait_recv()
@@ -1655,13 +1747,18 @@
 
     lax.fori_loop(0, 4, first_grad, 0)
     fold_f.open([first_g])
-    fold_m.cross()
+    for k in (2, 1, 3):
+        project(wrap(y + k))
+        y_send_buf[k - 1] = hidden_grad[...].astype(BF16)
+        grad_copy(k).start()
+
     tally.finish(0)
     tally.start(1)
+    for d in (2, 1, 3):
+        fold_f.add(d)
     project(y)
-    for d in (2, 1, 3, 0):
-        fold_f.add(d)
     fold_f.relay()
+    fold_f.add(0)
     for k in (1, 2, 3):
         grad_copy(k).wait_recv()
         hidden_grad[...] += y_got_buf[k - 1].astype(F32)
@@ -1693,9 +1790,14 @@
         hand_one.wait_send()
         one.wait_send()
 
+    @pl.when((x == 0) | (x == 3))
+    def _():
+        part_on.wait_send()
+
     @pl.when(x > 1)
     def _():
-        two.wait_send()
+        part_a.wait_send()
+        part_b.wait_send()
 
         @pl.when(c == 0)
         def _():
@@ -1729,8 +1831,11 @@
             VMEM((HEADS, 64, ROWS), F32),
             VMEM((5 * ROWS, 2 * COLS), BF16),
         ]
-        + [block] * 7
+        + [block] * 5
         + [
+            VMEM((ROWS - UP, 2 * COLS), BF16),
+            VMEM((UP, 2 * COLS), BF16),
+            VMEM((ROWS - UP, 2 * COLS), BF16),
             VMEM((ROWS, 2 * COLS), F32),
             VMEM((ROWS, D), BF16),
             VMEM((D, 384), F32),
@@ -1743,8 +1848,8 @@
             VMEM((3, 40, D), F32),
             VMEM((1, 40, D), F32),
             DMA((9,)),
-            DMA((5,)),
-            DMA((5,)),
+            DMA((7,)),
+            DMA((7,)),
             DMA((4,)),
             DMA((4,)),
             DMA((4,)),

time: 253 us -> 244 us (0.964)
  Pallas kernels: 252 us -> 243 us
    pallas_call x1, Pallas kernels: 75.2 us -> 70.4 us  [front(): pl.pallas_call(front_kernel, out_shape=tuple((o[0] for o in outs)), in_sp...]
    pallas_call x1, Pallas kernels: 97.7 us -> 94.4 us  [tail(): pl.pallas_call(tail_kernel, out_shape=tuple((sds(s, F32) for s in shapes)...]
where the time goes in v3:
time: 244 us
  Pallas kernels  243 us (100%)
    pallas_call x1, Pallas kernels, tail(): pl.pallas_call(tail_kernel, out_shape=tuple((sds(s, F32) for s in shapes)...  94.4 us
    pallas_call x1, Pallas kernels, middle(): pl.pallas_call(middle_kernel, out_shape=(sds((COLS, ROWS), BF16), sds((TO...  75.8 us
    pallas_call x1, Pallas kernels, front(): pl.pallas_call(front_kernel, out_shape=tuple((o[0] for o in outs)), in_sp...  70.4 us

profile of v3, /device:TPU:1, one launch (start us, length us, event | category | flops | bytes accessed | tf_op | source)
XLA Modules:
  0.0 244.2 jit_solution(5211894515155209438)
XLA Ops:
  0.7 70.4 %front.1 = (bf16[1280,512]{1,0:T(8,128)(2,1)}, bf16[128,1280]{1,0:T(8,128)(2,1)}, bf16[128,1280]{1,0:T(8,128)(2,1)}, f32[2,1280]{1,0:T(2,128)}, f32[8,128]{1,0:T...) custom-call(bf16[320,512]{1,0:T(8,128)(2,1)} %bitcast.15, ...), custom_call_target="tpu_custom_call" | custom-call | tf_op jit(solution)/shard_map/front/pallas_call | solution.py:760
  71.1 75.8 %middle.1 = (bf16[320,512]{1,0:T(8,128)(2,1)}, bf16[128,1280]{1,0:T(8,128)(2,1)}, f32[1280,128]{1,0:T(8,128)}, f32[8,1280]{1,0:T(8,128)}, bf16[1280,1280]{1,0:T(...) custom-call(bf16[512,384]{1,0:T(8,128)(2,1)} %get-tuple-element.66.att, ...), custom_call_target="tpu_custom_call" | custom-call | tf_op jit(solution)/shard_map/middle/pallas_call | solution.py:1192
  146.8 94.4 %tail.1 = (f32[320,512]{1,0:T(8,128)}, f32[40,320]{1,0:T(8,128)}, f32[40,320]{1,0:T(8,128)}, f32[40,320]{1,0:T(8,128)}, f32[40,320]{1,0:T(8,128)}, /*index=5*/f3...) custom-call(s32[1,512]{1,0:T(1,128)} %get-tuple-element.62.starts, ...), custom_call_target="tpu_custom_call" | custom-call | tf_op jit(solution)/shard_map/tail/pallas_call | solution.py:1817
  241.2 2.8 %emit.1 = (bf16[320,512]{1,0:T(8,128)(2,1)}, f32[320,512]{1,0:T(8,128)}, f32[40,320]{1,0:T(8,128)}, f32[40,320]{1,0:T(8,128)}, f32[40,320]{1,0:T(8,128)}, /*inde...) custom-call(f32[8,1280]{1,0:T(8,128)} %get-tuple-element.84.sums, ...), custom_call_target="tpu_custom_call" | custom-call | tf_op jit(solution)/shard_map/emit/pallas_call | solution.py:1884

commit v4 on v3

--- a/solution.py
+++ b/solution.py
@@ -1459,6 +1459,7 @@
     side_got,
     sums,
     m_out,
+    n_out,
     f_out,
     in_sem,
     k_send,
@@ -1472,6 +1473,7 @@
     *rest,
 ):
     m_bufs, m_sems, rest = rest[:7], rest[7:16], rest[16:]
+    n_bufs, n_sems, rest = rest[:7], rest[7:16], rest[16:]
     f_bufs, f_sems, rest = rest[:7], rest[7:16], rest[16:]
     t_accs, t_parts, t_send, t_recv = rest
     z, x, c, y = spot()
@@ -1496,12 +1498,14 @@
     ]
     meet(across + tally.peers[0] + tally.peers[1] + tally.peers[2])
     fold_m = Fold(m_bufs, m_sems, True)
+    fold_n = Fold(n_bufs, n_sems, False)
     fold_f = Fold(f_bufs, f_sems, False)
     my_rows = pl.ds(pl.multiple_of(TOK * y, TOK), TOK)
     attn[my_rows, :] = attn_low[...]
     spread = Spread(attn, g_send, g_recv)
     spread.start()
-    fold_m.open([m0, m1, m2])
+    fold_m.open([m0, m1])
+    fold_n.open([m2])
     for load in loads:
         load.start()
     side_src[...] = jnp.zeros_like(side_src)
@@ -1523,11 +1527,14 @@
 
     unproject(0)
     fold_m.add(2)
+    fold_n.add(2)
     spread.sides()
     fold_m.add(1)
+    fold_n.add(1)
     unproject(1)
     unproject(3)
     fold_m.add(3)
+    fold_n.add(3)
     spread.opposite()
     unproject(2)
 
@@ -1659,6 +1666,7 @@
             @pl.when(i == n)
             def _(d=d):
                 fold_m.add(d)
+                fold_n.add(d)
 
         @pl.when((i == 6) & ((x == 0) | (x == 3)))
         def _():
@@ -1668,6 +1676,7 @@
         @pl.when(i == 5)
         def _():
             fold_m.relay()
+            fold_n.relay()
 
         return carry
 
@@ -1688,6 +1697,7 @@
     out_part[...] = dot_tn(attn[...], att[...])
 
     fold_m.cross()
+    fold_n.cross()
     kv_sum[...] = d_win[4 * ROWS :, :].astype(F32)
 
     @pl.when(c == 0)
@@ -1765,14 +1775,16 @@
     tally.finish(1)
     tally.start(2)
     fold_m.finish(m_out)
+    fold_n.finish(n_out)
     fold_f.cross()
     fold_f.finish(f_out)
     tally.finish(2)
     fold_m.close(m_out)
+    fold_n.close(n_out)
     fold_f.close(f_out)
     gate_g[...] = m_out[0]
     up_g[...] = m_out[1]
-    down_g[...] = m_out[2]
+    down_g[...] = n_out[0]
     query_g[:, 0:256] = f_out[0, :, 384:640]
     query_g[:, 256:320] = f_out[0, :, 0:64]
     key_g[...] = f_out[0, :, 640:960]
@@ -1845,7 +1857,8 @@
             VMEM((4, 8, 384), F32),
             VMEM((4, 8, 384), F32),
             VMEM((8, D), F32),
-            VMEM((3, 40, D), F32),
+            VMEM((2, 40, D), F32),
+            VMEM((1, 40, D), F32),
             VMEM((1, 40, D), F32),
             DMA((9,)),
             DMA((7,)),
@@ -1857,7 +1870,8 @@
             DMA((4,)),
             DMA((4,)),
         ]
-        + fold_scratch(3)
+        + fold_scratch(2)
+        + fold_scratch(1)
         + fold_scratch(1)
         + tally_scratch((8, D)),
         compiler_params=params(2),

time: 244 us -> 242 us (level)
  Pallas kernels: 243 us -> 240 us
    pallas_call x1, Pallas kernels: 94.4 us -> 91.2 us  [tail(): pl.pallas_call(tail_kernel, out_shape=tuple((sds(s, F32) for s in shapes)...]
where the time goes in v4:
time: 242 us; the launch traced here: 241 us
  Pallas kernels  240 us (99%)
    pallas_call x1, Pallas kernels, tail(): pl.pallas_call(tail_kernel, out_shape=tuple((sds(s, F32) for s in shapes)...  91.2 us
    pallas_call x1, Pallas kernels, middle(): pl.pallas_call(middle_kernel, out_shape=(sds((COLS, ROWS), BF16), sds((TO...  75.8 us
    pallas_call x1, Pallas kernels, front(): pl.pallas_call(front_kernel, out_shape=tuple((o[0] for o in outs)), in_sp...  70.4 us

profile of v4, /device:TPU:1, one launch (start us, length us, event | category | flops | bytes accessed | tf_op | source)
XLA Modules:
  0.0 241.0 jit_solution(6974432956280995760)
XLA Ops:
  0.7 70.4 %front.1 = (bf16[1280,512]{1,0:T(8,128)(2,1)}, bf16[128,1280]{1,0:T(8,128)(2,1)}, bf16[128,1280]{1,0:T(8,128)(2,1)}, f32[2,1280]{1,0:T(2,128)}, f32[8,128]{1,0:T...) custom-call(bf16[320,512]{1,0:T(8,128)(2,1)} %bitcast.15, ...), custom_call_target="tpu_custom_call" | custom-call | tf_op jit(solution)/shard_map/front/pallas_call | solution.py:760
  71.1 75.8 %middle.1 = (bf16[320,512]{1,0:T(8,128)(2,1)}, bf16[128,1280]{1,0:T(8,128)(2,1)}, f32[1280,128]{1,0:T(8,128)}, f32[8,1280]{1,0:T(8,128)}, bf16[1280,1280]{1,0:T(...) custom-call(bf16[512,384]{1,0:T(8,128)(2,1)} %get-tuple-element.66.att, ...), custom_call_target="tpu_custom_call" | custom-call | tf_op jit(solution)/shard_map/middle/pallas_call | solution.py:1192
  146.8 91.2 %tail.1 = (f32[320,512]{1,0:T(8,128)}, f32[40,320]{1,0:T(8,128)}, f32[40,320]{1,0:T(8,128)}, f32[40,320]{1,0:T(8,128)}, f32[40,320]{1,0:T(8,128)}, /*index=5*/f3...) custom-call(s32[1,512]{1,0:T(1,128)} %get-tuple-element.62.starts, ...), custom_call_target="tpu_custom_call" | custom-call | tf_op jit(solution)/shard_map/tail/pallas_call | solution.py:1829
  238.0 2.8 %emit.1 = (bf16[320,512]{1,0:T(8,128)(2,1)}, f32[320,512]{1,0:T(8,128)}, f32[40,320]{1,0:T(8,128)}, f32[40,320]{1,0:T(8,128)}, f32[40,320]{1,0:T(8,128)}, /*inde...) custom-call(f32[8,1280]{1,0:T(8,128)} %get-tuple-element.84.sums, ...), custom_call_target="tpu_custom_call" | custom-call | tf_op jit(solution)/shard_map/emit/pallas_call | solution.py:1898

commit v5 on v4

--- a/solution.py
+++ b/solution.py
@@ -1675,8 +1675,8 @@
 
         @pl.when(i == 5)
         def _():
+            fold_n.relay()
             fold_m.relay()
-            fold_n.relay()
 
         return carry
 
@@ -1696,8 +1696,8 @@
         gain_parts.append(gain_part)
     out_part[...] = dot_tn(attn[...], att[...])
 
+    fold_n.cross()
     fold_m.cross()
-    fold_n.cross()
     kv_sum[...] = d_win[4 * ROWS :, :].astype(F32)
 
     @pl.when(c == 0)

time: 242 us -> 242 us (level)
  no operation moved by 1% of the time
where the time goes in v5:
time: 242 us; the launch traced here: 241 us
  Pallas kernels  240 us (99%)
    pallas_call x1, Pallas kernels, tail(): pl.pallas_call(tail_kernel, out_shape=tuple((sds(s, F32) for s in shapes)...  91.3 us
    pallas_call x1, Pallas kernels, middle(): pl.pallas_call(middle_kernel, out_shape=(sds((COLS, ROWS), BF16), sds((TO...  75.8 us
    pallas_call x1, Pallas kernels, front(): pl.pallas_call(front_kernel, out_shape=tuple((o[0] for o in outs)), in_sp...  70.4 us

profile of v5, /device:TPU:1, one launch (start us, length us, event | category | flops | bytes accessed | tf_op | source)
XLA Modules:
  0.0 241.1 jit_solution(7940622627911452080)
XLA Ops:
  0.7 70.4 %front.1 = (bf16[1280,512]{1,0:T(8,128)(2,1)}, bf16[128,1280]{1,0:T(8,128)(2,1)}, bf16[128,1280]{1,0:T(8,128)(2,1)}, f32[2,1280]{1,0:T(2,128)}, f32[8,128]{1,0:T...) custom-call(bf16[320,512]{1,0:T(8,128)(2,1)} %bitcast.15, ...), custom_call_target="tpu_custom_call" | custom-call | tf_op jit(solution)/shard_map/front/pallas_call | solution.py:760
  71.1 75.8 %middle.1 = (bf16[320,512]{1,0:T(8,128)(2,1)}, bf16[128,1280]{1,0:T(8,128)(2,1)}, f32[1280,128]{1,0:T(8,128)}, f32[8,1280]{1,0:T(8,128)}, bf16[1280,1280]{1,0:T(...) custom-call(bf16[512,384]{1,0:T(8,128)(2,1)} %get-tuple-element.66.att, ...), custom_call_target="tpu_custom_call" | custom-call | tf_op jit(solution)/shard_map/middle/pallas_call | solution.py:1192
  146.8 91.3 %tail.1 = (f32[320,512]{1,0:T(8,128)}, f32[40,320]{1,0:T(8,128)}, f32[40,320]{1,0:T(8,128)}, f32[40,320]{1,0:T(8,128)}, f32[40,320]{1,0:T(8,128)}, /*index=5*/f3...) custom-call(s32[1,512]{1,0:T(1,128)} %get-tuple-element.62.starts, ...), custom_call_target="tpu_custom_call" | custom-call | tf_op jit(solution)/shard_map/tail/pallas_call | solution.py:1829
  238.1 2.8 %emit.1 = (bf16[320,512]{1,0:T(8,128)(2,1)}, f32[320,512]{1,0:T(8,128)}, f32[40,320]{1,0:T(8,128)}, f32[40,320]{1,0:T(8,128)}, f32[40,320]{1,0:T(8,128)}, /*inde...) custom-call(f32[8,1280]{1,0:T(8,128)} %get-tuple-element.84.sums, ...), custom_call_target="tpu_custom_call" | custom-call | tf_op jit(solution)/shard_map/emit/pallas_call | solution.py:1898
